TPU v7x, 32 devices: a whole 2x2x4 slice. The times are simulated.
32 devices in a mesh: parts: 2 (over y), tensor: 4 (over z), fsdp: 4 (over x, core).
Axes of the slice: x: 2, y: 2, z: 4, core: 2. Of those that a mesh axis runs over, the one named last changes fastest.
Arguments:
- tokens: bfloat16 [1024, 4096], P(('parts', 'fsdp'), 'tensor'), parts along dimension 0, may hold values from -6 to 6
- cotangent: bfloat16 [1024, 4096], P(('parts', 'fsdp'), 'tensor'), parts along dimension 0, may hold values from -6 to 6
- gate_values: bfloat16 [8, 160, 128, 128], P('fsdp', 'tensor'), may hold values from -0.1875 to 0.1875
- gate_rows: int32 [8, 160], P('fsdp', 'tensor'), may hold values from 0 to 31, as said below
- gate_scale: bfloat16 [8, 160], P('fsdp', 'tensor'), may hold values from 0.5 to 2
- up_values: bfloat16 [8, 160, 128, 128], P('fsdp', 'tensor'), may hold values from -0.1875 to 0.1875
- up_rows: int32 [8, 160], P('fsdp', 'tensor'), may hold values from 0 to 31, as said below
- up_scale: bfloat16 [8, 160], P('fsdp', 'tensor'), may hold values from 0.5 to 2
- down_values: bfloat16 [8, 160, 128, 128], P('fsdp', 'tensor'), may hold values from -0.078125 to 0.078125
- down_cols: int32 [8, 160], P('fsdp', 'tensor'), may hold values from 0 to 31, as said below
- down_scale: bfloat16 [8, 160], P('fsdp', 'tensor'), may hold values from 0.5 to 2
Outputs:
- layer_out: bfloat16 [1024, 4096], P(('parts', 'fsdp'), 'tensor'), parts along dimension 0
- grad_tokens: bfloat16 [1024, 4096], P(('parts', 'fsdp'), 'tensor'), parts along dimension 0
- grad_gate: bfloat16 [16, 160, 128, 128], P(('parts', 'fsdp'), 'tensor'), parts along dimension 0
- grad_up: bfloat16 [16, 160, 128, 128], P(('parts', 'fsdp'), 'tensor'), parts along dimension 0
- grad_down: bfloat16 [16, 160, 128, 128], P(('parts', 'fsdp'), 'tensor'), parts along dimension 0
There are 2 independent parts, one for each index of `parts`. A program takes and returns all parts, laid end to end along the dimension named above; an argument that names none is the same for every part. Nothing has to cross between parts.
Inputs may be any that keep to these rules, and one draw needn't show every extreme that they name: `gate_rows`: the 8 entries of each column name distinct input blocks; some input blocks are named far more often than others. `up_rows`: the 8 entries of each column name distinct input blocks; some input blocks are named far more often than others. `down_cols`: the 8 entries of each column name distinct output blocks; some output blocks are named far more often than others.
All inputs are finite; a program needn't handle non-finite values.
Results may differ from a plain program's by a relative error of at most 0.023.
Values may be sent and summed in bfloat16 or wider, within the bound.
A program may use at most 192 MiB of HBM per device.

v0:
```python
import functools

import jax
import jax.numpy as jnp
from jax import lax
from jax.experimental import pallas as pl
from jax.experimental.pallas import tpu as pltpu
from jax.sharding import PartitionSpec as P


def scaled_sum(products, factors):
    return jnp.sum(products * factors.astype(jnp.float32)[None, :, :, None], axis=1)


def slot_term(selected, grads, factors):
    return (
        jnp.einsum("tkra,trb->krab", selected, grads, preferred_element_type=jnp.float32)
        * factors[:, :, None, None]
    )


def gathered_plan(
    tokens,
    cotangent,
    gate_values,
    gate_rows,
    gate_scale,
    up_values,
    up_rows,
    up_scale,
    down_values,
    down_cols,
    down_scale,
):
    block_size = gate_values.shape[-1]
    token_count = tokens.shape[0]
    tensor_count = lax.axis_size("tensor")
    nblocks = tokens.shape[1] * tensor_count // block_size
    local_blocks = nblocks // tensor_count
    gathered = lax.all_gather(tokens, "tensor", axis=1, tiled=True)
    x_blocks = gathered.reshape(token_count, nblocks, block_size)
    gate_where, up_where, down_where = (
        lax.all_gather(gate_rows, "fsdp", axis=0, tiled=True),
        lax.all_gather(up_rows, "fsdp", axis=0, tiled=True),
        lax.all_gather(down_cols, "fsdp", axis=0, tiled=True),
    )
    gate_blocks, gate_factor, up_blocks, up_factor, down_blocks, down_factor = (
        lax.all_gather(gate_values, "fsdp", axis=0, tiled=True),
        lax.all_gather(gate_scale, "fsdp", axis=0, tiled=True),
        lax.all_gather(up_values, "fsdp", axis=0, tiled=True),
        lax.all_gather(up_scale, "fsdp", axis=0, tiled=True),
        lax.all_gather(down_values, "fsdp", axis=0, tiled=True),
        lax.all_gather(down_scale, "fsdp", axis=0, tiled=True),
    )
    gate_sel = x_blocks[:, gate_where]
    up_sel = x_blocks[:, up_where]
    gate_pre = scaled_sum(
        jnp.einsum("tkra,krab->tkrb", gate_sel, gate_blocks, preferred_element_type=jnp.float32),
        gate_factor,
    )
    up_pre = scaled_sum(
        jnp.einsum("tkra,krab->tkrb", up_sel, up_blocks, preferred_element_type=jnp.float32),
        up_factor,
    )
    sigmoid_gate = jax.nn.sigmoid(gate_pre)
    activated = gate_pre * sigmoid_gate
    hidden = (activated * up_pre).astype(jnp.bfloat16)
    down_float = down_factor.astype(jnp.float32)
    down_scaled = (
        jnp.einsum("trb,krbc->krtc", hidden, down_blocks, preferred_element_type=jnp.float32)
        * down_float[:, :, None, None]
    )
    out_full = (
        jnp.zeros((nblocks, token_count, block_size), jnp.float32).at[down_where].add(down_scaled)
    )
    out_part = lax.psum_scatter(
        out_full.astype(jnp.bfloat16), "tensor", scatter_dimension=0, tiled=True
    ).astype(jnp.float32)
    layer_out = (
        jnp.transpose(out_part, (1, 0, 2))
        .reshape(token_count, local_blocks * block_size)
        .astype(jnp.bfloat16)
    )
    grad_full = lax.all_gather(cotangent, "tensor", axis=1, tiled=True).reshape(
        token_count, nblocks, block_size
    )
    down_sel = grad_full[:, down_where]
    gate_float = gate_factor.astype(jnp.float32)
    up_float = up_factor.astype(jnp.float32)
    grad_hidden = scaled_sum(
        jnp.einsum("tkrc,krbc->tkrb", down_sel, down_blocks, preferred_element_type=jnp.float32),
        down_factor,
    )
    grad_down = lax.psum_scatter(
        (
            jnp.einsum("trb,tkrc->krbc", hidden, down_sel, preferred_element_type=jnp.float32)
            * down_float[:, :, None, None]
        ).astype(jnp.bfloat16),
        "fsdp",
        scatter_dimension=0,
        tiled=True,
    )
    grad_gate_act = (
        grad_hidden * up_pre * sigmoid_gate * (1.0 + gate_pre * (1.0 - sigmoid_gate))
    ).astype(jnp.bfloat16)
    grad_up_act = (grad_hidden * activated).astype(jnp.bfloat16)
    grad_gate = lax.psum_scatter(
        slot_term(gate_sel, grad_gate_act, gate_float).astype(jnp.bfloat16),
        "fsdp",
        scatter_dimension=0,
        tiled=True,
    )
    grad_up = lax.psum_scatter(
        slot_term(up_sel, grad_up_act, up_float).astype(jnp.bfloat16),
        "fsdp",
        scatter_dimension=0,
        tiled=True,
    )
    back_gate = (
        jnp.einsum("trb,krab->krta", grad_gate_act, gate_blocks, preferred_element_type=jnp.float32)
        * gate_float[:, :, None, None]
    )
    back_up = (
        jnp.einsum("trb,krab->krta", grad_up_act, up_blocks, preferred_element_type=jnp.float32)
        * up_float[:, :, None, None]
    )
    in_full = (
        jnp.zeros((nblocks, token_count, block_size), jnp.float32)
        .at[gate_where]
        .add(back_gate)
        .at[up_where]
        .add(back_up)
    )
    in_part = lax.psum_scatter(
        in_full.astype(jnp.bfloat16), "tensor", scatter_dimension=0, tiled=True
    ).astype(jnp.float32)
    grad_tokens = (
        jnp.transpose(in_part, (1, 0, 2))
        .reshape(token_count, local_blocks * block_size)
        .astype(jnp.bfloat16)
    )
    return (layer_out, grad_tokens, grad_gate, grad_up, grad_down)


def gather_kernel(shards, small, both, wg, wu, wd, tok_all, rg, ru, rd, table, *sems):
    (z_send, z_recv, c_send, c_recv, x_send, x_recv, w_send, w_recv, y_send, y_recv, n_send, n_recv, s_send, s_recv, here) = sems
    part, t, f = lax.axis_index("parts"), lax.axis_index("tensor"), lax.axis_index("fsdp")
    flip = [f, (f // 2) * 2 + 1 - f % 2, (f + 2) % 4, ((f + 2) % 4 // 2) * 2 + 1 - f % 2]
    count = rg.shape[2]
    last = shards - 1
    weights = ((wg, rg), (wu, ru), (wd, rd))

    def to(where, src, dst, send, recv):
        return pltpu.make_async_remote_copy(
            src_ref=src, dst_ref=dst, send_sem=send, recv_sem=recv,
            device_id=where, device_id_type=pl.DeviceIdType.MESH,
        )

    def across(m):
        return (part, t, flip[m])

    over = (1 - part, t, f)
    ups = ((part, t + 1, f), (part, t - 1, f))
    more = (t < last, t > 0)

    barrier = pltpu.get_barrier_semaphore()
    for m in (1, 2, 3):
        pl.semaphore_signal(barrier, inc=1, device_id=across(m), device_id_type=pl.DeviceIdType.MESH)
    pl.semaphore_signal(barrier, inc=1, device_id=over, device_id_type=pl.DeviceIdType.MESH)
    for way in range(2):
        @pl.when(more[way])
        def _():
            pl.semaphore_signal(barrier, inc=1, device_id=ups[way], device_id_type=pl.DeviceIdType.MESH)
    ends = jnp.logical_or(t == 0, t == last)

    @pl.when(ends)
    def _():
        pl.semaphore_wait(barrier, 5)

    @pl.when(jnp.logical_not(ends))
    def _():
        pl.semaphore_wait(barrier, 6)

    def z_copy(way, src, x, own=False):
        source = both if own else tok_all.at[0, src, x]
        return to(ups[way], source, tok_all.at[0, src, x], z_send.at[way, src, x], z_recv.at[way, src, x])

    def c_copy(src, x, own=False):
        source = both if own else tok_all.at[0, src, x]
        return to(across(1), source, tok_all.at[1, src, x], c_send.at[src, x], c_recv.at[src, x])

    x_copy = to(across(2), both, tok_all.at[0, t, 1], x_send, x_recv)
    keep = pltpu.make_async_copy(both, tok_all.at[0, t, 0], here)
    x_copy.start()
    for way in range(2):
        @pl.when(more[way])
        def _():
            z_copy(way, t, 0, True).start()
    tables = [
        to(across(m), small.at[flip[m]], table.at[m - 1], s_send.at[m - 1], s_recv.at[m - 1])
        for m in (1, 2, 3)
    ]
    for c in tables:
        c.start()
    c_copy(t, 0, True).start()
    w_copies, y_copies, y_waits, n_copies = [], [], [], []
    for w, r in weights:
        for m in (2, 3):
            j = len(w_copies)
            w_copies.append(to(across(m), w.at[part, pl.ds(flip[m] * count, count)], r.at[m - 1, part], w_send.at[j], w_recv.at[j]))
            y_copies.append(to(over, r.at[m - 1, part], r.at[m - 1, part], y_send.at[j], y_recv.at[j]))
            y_waits.append(to(over, r.at[m - 1, part], r.at[m - 1, 1 - part], y_send.at[j], y_recv.at[j]))
        for k in range(2):
            j = len(n_copies)
            n_copies.append(to(across(1), w.at[k, pl.ds(flip[1] * count, count)], r.at[0, k], n_send.at[j], n_recv.at[j]))
    for c in w_copies:
        c.start()
    for c in n_copies:
        c.start()
    keep.start()

    x_copy.wait_recv()
    for way in range(2):
        @pl.when(more[way])
        def _():
            z_copy(way, t, 1).start()
    c_copy(t, 1).start()

    def arrive(step, x):
        for way in range(2):
            src = t - step if way == 0 else t + step

            @pl.when(src >= 0 if way == 0 else src <= last)
            def _():
                z_copy(way, src, x).wait_recv()

                @pl.when(more[way])
                def _():
                    z_copy(way, src, x).start()

                c_copy(src, x).start()

    def relay(j):
        w_copies[j].wait_recv()
        y_copies[j].start()

    order = [(s, x) for s in range(1, shards) for x in range(2)]
    done = 0
    for i, (s, x) in enumerate(order):
        arrive(s, x)
        while done < len(w_copies) and done < 2 * i + 1:
            relay(done)
            done += 1
    while done < len(w_copies):
        relay(done)
        done += 1

    for way in range(2):
        for s in range(shards):
            src = t - s if way == 0 else t + s

            @pl.when(jnp.logical_and(src >= 0 if way == 0 else src <= last, more[way]))
            def _():
                for x in range(2):
                    z_copy(way, src, x, s == 0 and x == 0).wait_send()
    for src in range(shards):
        for x in range(2):
            c_copy(src, x).wait_send()
            c_copy(src, x).wait_recv()
    for c in tables + n_copies:
        c.wait_send()
        c.wait_recv()
    x_copy.wait_send()
    for c in w_copies + y_copies:
        c.wait_send()
    for c in y_waits:
        c.wait_recv()
    keep.wait()


def gather(small, both, weights, shards):
    per_dev, local_cols, blk, _ = weights[0].shape
    count = local_cols // 4
    bf = jnp.bfloat16
    dma = lambda *a: pltpu.SemaphoreType.DMA(a)
    received = jax.ShapeDtypeStruct((3, per_dev, count, blk, blk), bf)
    anywhere = pl.BlockSpec(memory_space=pl.ANY)
    z = (2, shards, 2)
    c = (shards, 2)
    one = pltpu.SemaphoreType.DMA
    return pl.pallas_call(
        functools.partial(gather_kernel, shards),
        out_shape=[
            jax.ShapeDtypeStruct((2, shards, 2) + both.shape, bf),
            received, received, received,
            jax.ShapeDtypeStruct((3,) + small.shape[1:], jnp.float32),
        ],
        in_specs=[anywhere] * 5,
        out_specs=[anywhere] * 5,
        scratch_shapes=[dma(*z), dma(*z), dma(*c), dma(*c), one, one, dma(6), dma(6), dma(6), dma(6), dma(6), dma(6), dma(3), dma(3), one],
        compiler_params=pltpu.CompilerParams(collective_id=0, has_side_effects=True),
    )(small, both, *weights)


NN = (((1,), (0,)), ((), ()))
NT = (((1,), (1,)), ((), ()))
dot = functools.partial(lax.dot_general, preferred_element_type=jnp.float32)


def load(rows_ref, tok_ref, tok, which, array, slot, sel):
    per_shard, blk = tok_ref.shape[4], tok_ref.shape[6]
    place = rows_ref[array, slot, pl.program_id(0)]
    shard, block = place // per_shard, place % per_shard
    for c in range(2):
        for x in range(2):
            q = c * 2 + x
            sel[q * tok : (q + 1) * tok, slot * blk : (slot + 1) * blk] = tok_ref[c, shard, x, which, block]


def scaled(scale_ref, own, recv, array, slot):
    per_dev = own.shape[0]
    src, sub = slot // per_dev, slot % per_dev
    value = recv[src - 1, sub, 0] if src else own[sub, 0]
    return (value.astype(jnp.float32) * scale_ref[array, slot, pl.program_id(0)]).astype(jnp.bfloat16)


def accumulate(rows_ref, acc, array, slots, blk, product):
    for slot in range(slots):
        acc[rows_ref[array, slot, pl.program_id(0)]] += product[:, slot * blk : (slot + 1) * blk]


def clear(acc):
    @pl.when(pl.program_id(0) == 0)
    def _():
        acc[...] = jnp.zeros_like(acc)


def flush(place_ref, acc, tok, own, other):
    per_shard = own[0].shape[1]

    @pl.when(pl.program_id(0) == pl.num_programs(0) - 1)
    def _():
        for m in range(len(own)):
            first = (place_ref[1] ^ m) * per_shard
            for c, ref in enumerate((own[m], other[m])):
                for x in range(2):
                    q = c * 2 + x

                    @pl.loop(0, per_shard)
                    def _(d):
                        ref[x, d] = acc[first + d, q * tok : (q + 1) * tok, :].astype(jnp.bfloat16)


def early_kernel(dims, rows_ref, scale_ref, place_ref, tok_ref, *refs):
    slots, per_dev, tok, blk, shards = dims
    nsrc = slots // per_dev
    own_w, recv_w, refs = refs[:3], refs[3:6], refs[6:]
    grads, (gate_pre_ref, up_pre_ref), refs = refs[:nsrc], refs[nsrc : nsrc + 2], refs[nsrc + 2 :]
    own, other, scratch = refs[:shards], refs[shards : 2 * shards], refs[2 * shards :]
    acc, gate_sel, up_sel, down_sel, gate_w, up_w, down_w = scratch
    r = pl.program_id(0)
    clear(acc)
    for slot in range(slots):
        span = slice(slot * blk, (slot + 1) * blk)
        load(rows_ref, tok_ref, tok, 0, 0, slot, gate_sel)
        load(rows_ref, tok_ref, tok, 0, 1, slot, up_sel)
        load(rows_ref, tok_ref, tok, 1, 2, slot, down_sel)
        gate_w[span, :] = scaled(scale_ref, own_w[0], recv_w[0], 0, slot)
        up_w[span, :] = scaled(scale_ref, own_w[1], recv_w[1], 1, slot)
        down_w[:, span] = scaled(scale_ref, own_w[2], recv_w[2], 2, slot)
    gate_pre = dot(gate_sel[...], gate_w[...], NN)
    up_pre = dot(up_sel[...], up_w[...], NN)
    gate_pre_ref[0], up_pre_ref[0] = gate_pre, up_pre
    hidden = (gate_pre * jax.nn.sigmoid(gate_pre) * up_pre).astype(jnp.bfloat16)
    down = dot(hidden.T, down_sel[...], NN)
    for slot in range(slots):
        src, sub = slot // per_dev, slot % per_dev
        g = down[:, slot * blk : (slot + 1) * blk] * scale_ref[2, slot, r]
        grads[src][sub, 0] = g.astype(jnp.bfloat16)
    accumulate(rows_ref, acc, 2, slots, blk, dot(hidden, down_w[...], NN))
    flush(place_ref, acc, tok, own, other)


def middle_kernel(dims, rows_ref, scale_ref, place_ref, tok_ref, own_w, recv_w, gate_pre_ref, up_pre_ref, *refs):
    slots, per_dev, tok, blk, _ = dims
    nsrc = slots // per_dev
    grads, (gate_act_ref, up_act_ref), scratch = (refs[:nsrc], refs[nsrc : 2 * nsrc]), refs[2 * nsrc : 2 * nsrc + 2], refs[2 * nsrc + 2 :]
    gate_sel, up_sel, down_sel, down_w = scratch
    r = pl.program_id(0)
    for slot in range(slots):
        load(rows_ref, tok_ref, tok, 0, 0, slot, gate_sel)
        load(rows_ref, tok_ref, tok, 0, 1, slot, up_sel)
        load(rows_ref, tok_ref, tok, 1, 2, slot, down_sel)
        down_w[:, slot * blk : (slot + 1) * blk] = scaled(scale_ref, own_w, recv_w, 2, slot)
    gate_pre, up_pre = gate_pre_ref[0], up_pre_ref[0]
    grad_hidden = dot(down_sel[...], down_w[...], NT)
    sig = jax.nn.sigmoid(gate_pre)
    act = gate_pre * sig
    gate_act = (grad_hidden * up_pre * sig * (1.0 + gate_pre * (1.0 - sig))).astype(jnp.bfloat16)
    up_act = (grad_hidden * act).astype(jnp.bfloat16)
    gate_act_ref[0], up_act_ref[0] = gate_act, up_act
    for slot in range(slots):
        span = slice(slot * blk, (slot + 1) * blk)
        src, sub = slot // per_dev, slot % per_dev
        g = dot(gate_sel[:, span].T, gate_act, NN) * scale_ref[0, slot, r]
        grads[0][src][sub, 0] = g.astype(jnp.bfloat16)
        g = dot(up_sel[:, span].T, up_act, NN) * scale_ref[1, slot, r]
        grads[1][src][sub, 0] = g.astype(jnp.bfloat16)


def late_kernel(dims, rows_ref, scale_ref, place_ref, *refs):
    slots, _, tok, blk, shards = dims
    own_w, recv_w, (gate_act_ref, up_act_ref), refs = refs[:2], refs[2:4], refs[4:6], refs[6:]
    own, other, (acc, gate_w, up_w) = refs[:shards], refs[shards : 2 * shards], refs[2 * shards :]
    clear(acc)
    for slot in range(slots):
        span = slice(slot * blk, (slot + 1) * blk)
        gate_w[span, :] = scaled(scale_ref, own_w[0], recv_w[0], 0, slot)
        up_w[span, :] = scaled(scale_ref, own_w[1], recv_w[1], 1, slot)
    accumulate(rows_ref, acc, 0, slots, blk, dot(gate_act_ref[0], gate_w[...], NT))
    accumulate(rows_ref, acc, 1, slots, blk, dot(up_act_ref[0], up_w[...], NT))
    flush(place_ref, acc, tok, own, other)


def columns(which, scalars, tok_all, own_w, recv_w, kept):
    nsrc = 1 + recv_w[0].shape[0]
    _, per_dev, count, blk, _ = recv_w[0].shape
    _, shards, _, _, per_shard, tok, _ = tok_all.shape
    nblk = shards * per_shard
    slots = per_dev * nsrc
    total = 4 * tok
    bf, f32 = jnp.bfloat16, jnp.float32
    whole = lambda a: pl.BlockSpec(a, lambda r, *_: (0,) * len(a), pipeline_mode=pl.Buffered(1))
    own_block = pl.BlockSpec((per_dev, 1, blk, blk), lambda r, rows, scale, at: (0, at[0] * count + r, 0, 0))
    recv_block = pl.BlockSpec((nsrc - 1, per_dev, 1, blk, blk), lambda r, *_: (0, 0, r, 0, 0))
    block = pl.BlockSpec((per_dev, 1, blk, blk), lambda r, *_: (0, r, 0, 0))
    piece = jax.ShapeDtypeStruct((per_dev, count, blk, blk), bf)
    kept_block = [pl.BlockSpec((1, total, blk), lambda r, *_: (r, 0, 0))] * 2
    keep = lambda kind: [jax.ShapeDtypeStruct((count, total, blk), kind)] * 2
    sum_block = [whole((2, per_shard, tok, blk))] * (2 * shards)
    sums = [jax.ShapeDtypeStruct((2, per_shard, tok, blk), bf)] * (2 * shards)
    acc = pltpu.VMEM((nblk, total, blk), f32)
    sel = pltpu.VMEM((total, slots * blk), bf)
    tall, wide = pltpu.VMEM((slots * blk, blk), bf), pltpu.VMEM((blk, slots * blk), bf)
    if which == "early":
        body, products = early_kernel, 4
        in_specs = [whole(tok_all.shape)] + [own_block] * 3 + [recv_block] * 3
        operands = (tok_all, *own_w, *recv_w)
        out_specs, out_shape = [block] * nsrc + kept_block + sum_block, [piece] * nsrc + keep(f32) + sums
        scratch = [acc, sel, sel, sel, tall, tall, wide]
    elif which == "middle":
        body, products = middle_kernel, 3
        in_specs = [whole(tok_all.shape), own_block, recv_block] + kept_block
        operands = (tok_all, own_w[2], recv_w[2], *kept)
        out_specs, out_shape = [block] * (2 * nsrc) + kept_block, [piece] * (2 * nsrc) + keep(bf)
        scratch = [sel, sel, sel, wide]
    else:
        body, products = late_kernel, 2
        in_specs = [own_block] * 2 + [recv_block] * 2 + kept_block
        operands = (*own_w[:2], *recv_w[:2], *kept)
        out_specs, out_shape = sum_block, sums
        scratch = [acc, tall, tall]
    flops = 2 * products * slots * count * total * blk * blk
    return pl.pallas_call(
        functools.partial(body, (slots, per_dev, tok, blk, shards)),
        grid_spec=pltpu.PrefetchScalarGridSpec(
            num_scalar_prefetch=3, grid=(count,), in_specs=in_specs, out_specs=out_specs, scratch_shapes=scratch,
        ),
        out_shape=out_shape,
        compiler_params=pltpu.CompilerParams(vmem_limit_bytes=60 * 1024 * 1024),
        cost_estimate=pl.CostEstimate(flops=flops, bytes_accessed=40 << 20, transcendentals=0),
    )(*scalars, *operands)


def swap(value, flip, axis="fsdp"):
    return lax.ppermute(value, axis, [(i, i ^ flip) for i in range(lax.axis_size(axis))])


def exchanged_plan(
    tokens,
    cotangent,
    gate_values,
    gate_rows,
    gate_scale,
    up_values,
    up_rows,
    up_scale,
    down_values,
    down_cols,
    down_scale,
):
    tok, width = tokens.shape
    per_dev, local_cols, blk, _ = gate_values.shape
    count = local_cols // 4
    mine, shard = lax.axis_index("fsdp"), lax.axis_index("tensor")
    f32, bf = jnp.float32, jnp.bfloat16

    shards = lax.axis_size("tensor")
    both = jnp.stack([tokens, cotangent]).reshape(2, tok, width // blk, blk).transpose(0, 2, 1, 3)
    small = jnp.stack(
        [a.astype(f32) for a in (gate_rows, up_rows, down_cols, gate_scale, up_scale, down_scale)]
    )
    small = small.reshape(6, per_dev, 4, count).transpose(2, 0, 1, 3)
    own_w = (gate_values, up_values, down_values)
    tok_all, *recv_w, table = gather(small, both, own_w, shards)
    kept = lax.dynamic_slice_in_dim(small, mine, 1, axis=0)
    table = jnp.concatenate([kept, table]).transpose(1, 0, 2, 3).reshape(6, 4 * per_dev, count)
    table_rows = table[:3].astype(jnp.int32)
    table_scale = table[3:]

    def home(pieces):
        result = jnp.zeros((per_dev, local_cols, blk, blk), bf)
        for m, part in enumerate(pieces):
            result = lax.dynamic_update_slice_in_dim(result, part, (mine ^ m) * count, axis=1)
        return result

    def send(pieces):
        return [p if m == 0 else swap(p, m) for m, p in enumerate(pieces)]

    def chip_sum(own, other):
        return [(a.astype(f32) + swap(b, 1).astype(f32)).astype(bf) for a, b in zip(own, other)]

    def scatter(chip):
        return [c if m == 0 else swap(c, m, "tensor") for m, c in enumerate(chip)]

    def finish(shares):
        far = sum(s[1].astype(f32) for s in shares).astype(bf)
        total = (sum(s[0].astype(f32) for s in shares) + swap(far, 2).astype(f32)).astype(bf)
        return total.transpose(1, 0, 2).reshape(tok, width)

    scalars = (table_rows, table_scale, jnp.stack([mine, shard]).astype(jnp.int32))
    early = columns("early", scalars, tok_all, own_w, recv_w, ())
    down_pieces, pre, own, other = early[:4], early[4:6], early[6 : 6 + shards], early[6 + shards :]
    chip = chip_sum(own, other)
    down_sent = send(down_pieces)
    chip, pre = lax.optimization_barrier((chip, pre))
    out_shares = scatter(chip)
    middle = columns("middle", scalars, tok_all, own_w, recv_w, pre)
    gate_sent, up_sent = send(middle[:4]), send(middle[4:8])
    late = columns("late", scalars, tok_all, own_w, recv_w, middle[8:])
    chip = chip_sum(late[:shards], late[shards:])
    in_shares = scatter(chip)
    return (finish(out_shares), finish(in_shares), home(gate_sent), home(up_sent), home(down_sent))


def choose_plan(mesh, *args):
    fits = mesh.shape["fsdp"] == 4 and mesh.shape["parts"] == 2 and args[2].shape[0] == 2
    fits = fits and args[2].shape[1] % 4 == 0 and mesh.shape["tensor"] in (2, 4, 8)
    plan = exchanged_plan if fits else gathered_plan
    return plan(*args)


def solution(mesh):
    plan = functools.partial(choose_plan, mesh)
    in_specs = (
        P(("parts", "fsdp"), "tensor"),
        P(("parts", "fsdp"), "tensor"),
        P("fsdp", "tensor", None, None),
        P("fsdp", "tensor"),
        P("fsdp", "tensor"),
        P("fsdp", "tensor", None, None),
        P("fsdp", "tensor"),
        P("fsdp", "tensor"),
        P("fsdp", "tensor", None, None),
        P("fsdp", "tensor"),
        P("fsdp", "tensor"),
    )
    out_specs = (
        P(("parts", "fsdp"), "tensor"),
        P(("parts", "fsdp"), "tensor"),
        P(("parts", "fsdp"), "tensor", None, None),
        P(("parts", "fsdp"), "tensor", None, None),
        P(("parts", "fsdp"), "tensor", None, None),
    )
    return jax.shard_map(plan, mesh=mesh, in_specs=in_specs, out_specs=out_specs, check_vma=False)
```

profile of v0, /device:TPU:0, one launch (start us, length us, event | category | flops | bytes accessed | tf_op | source)
XLA Modules:
  0.0 271.8 jit_solution(8051926913306659555)
XLA Ops:
  5.2 1.1 copy.47
  6.5 1.1 copy.46
  8.7 77.2 %shard_map.146 = (bf16[2,4,2,2,8,128,128]{6,5,4,3,2,1,0:T(8,128)(2,1)}, bf16[3,2,10,128,128]{4,3,2,1,0:T(8,128)(2,1)}, bf16[3,2,10,128,128]{4,3,2,1,0:T(8,128)(2...) custom-call(f32[4,6,2,10]{3,2,1,0:T(2,128)} %bitcast.45, bf16[2,8,128,128]{3,2,1,0:T(8,128)(2,1)} %maximum_bitcast_fusion.both, ...), custom_call_target="tpu_custom_call" | custom-call | tf_op jit(solution)/shard_map/pallas_call | solution.py:291
  88.6 25.5 %shard_map.147 = (bf16[2,10,128,128]{3,2,1,0:T(8,128)(2,1)}, bf16[2,10,128,128]{3,2,1,0:T(8,128)(2,1)}, bf16[2,10,128,128]{3,2,1,0:T(8,128)(2,1)}, bf16[2,10,128...) custom-call(s32[3,8,10]{2,1,0:T(8,128)} %bitcast.39, ...), custom_call_target="tpu_custom_call" | custom-call | flops 5368709120 | bytes 41943040 | tf_op jit(solution)/shard_map/pallas_call | solution.py:464
  116.5 1.5 collective-permute-start.23
  117.9 1.2 add_convert_fusion.7
  119.9 2.0 add_convert_fusion.6
  121.9 2.0 add_convert_fusion.5
  123.8 2.0 add_convert_fusion.4
  125.8 2.5 collective-permute-start.6
  128.3 26.3 %shard_map.148 = (bf16[2,10,128,128]{3,2,1,0:T(8,128)(2,1)}, bf16[2,10,128,128]{3,2,1,0:T(8,128)(2,1)}, bf16[2,10,128,128]{3,2,1,0:T(8,128)(2,1)}, bf16[2,10,128...) custom-call(s32[3,8,10]{2,1,0:T(8,128)} %bitcast.40, ...), custom_call_target="tpu_custom_call" | custom-call | flops 4026531840 | bytes 41943040 | tf_op jit(solution)/shard_map/pallas_call | solution.py:464
  154.6 16.4 %shard_map.149 = (bf16[2,8,128,128]{3,2,1,0:T(8,128)(2,1)}, bf16[2,8,128,128]{3,2,1,0:T(8,128)(2,1)}, bf16[2,8,128,128]{3,2,1,0:T(8,128)(2,1)}, bf16[2,8,128,128...) custom-call(s32[3,8,10]{2,1,0:T(8,128)} %bitcast.41, ...), custom_call_target="tpu_custom_call" | custom-call | flops 2684354560 | bytes 41943040 | tf_op jit(solution)/shard_map/pallas_call | solution.py:464
  174.4 1.3 constant_dynamic-update-slice_fusion.7
  176.0 1.2 constant_dynamic-update-slice_fusion.6
  178.2 1.7 collective-permute-start.4
  179.9 19.4 %collective-permute-done.5 = bf16[2,8,128,128]{3,2,1,0:T(8,128)(2,1)S(1)} collective-permute-done((bf16[2,8,128,128]{3,2,1,0:T(8,128)(2,1)S(1)}, bf16[2,8,128,128]{3,2,1,0:T(8,128)(2,1)S(1)}, u32[]{:S(2)}, u32[]{:S(2)}) %collective-permute-start.5) | collective-permute-done | bytes 524320 | tf_op jit(solution)/shard_map/ppermute | solution.py:476
  199.3 1.1 collective-permute-start.17
  201.8 1.8 collective-permute-done.4
  203.6 1.1 collective-permute-start.20
  204.7 1.1 fusion.2
  205.9 11.0 %collective-permute-done.17 = bf16[2,10,128,128]{3,2,1,0:T(8,128)(2,1)S(1)} collective-permute-done((bf16[2,10,128,128]{3,2,1,0:T(8,128)(2,1)S(1)}, bf16[2,10,128,128]{3,2,1,0:T(8,128)(2,1)S(1)}, u32[]{:S(2)}, u32[]{:S(2)}) %collective-permute-start.17) | collective-permute-done | bytes 655392 | tf_op jit(solution)/shard_map/ppermute | solution.py:476
  216.9 2.5 collective-permute-start.14
  219.4 10.2 %collective-permute-done.18 = bf16[2,10,128,128]{3,2,1,0:T(8,128)(2,1)S(1)} collective-permute-done((bf16[2,10,128,128]{3,2,1,0:T(8,128)(2,1)S(1)}, bf16[2,10,128,128]{3,2,1,0:T(8,128)(2,1)S(1)}, u32[]{:S(2)}, u32[]{:S(2)}) %collective-permute-start.18) | collective-permute-done | bytes 655392 | tf_op jit(solution)/shard_map/ppermute | solution.py:476
  229.6 3.0 %collective-permute-start.10 = (bf16[2,8,128,128]{3,2,1,0:T(8,128)(2,1)S(1)}, bf16[2,8,128,128]{3,2,1,0:T(8,128)(2,1)S(1)}, u32[]{:S(2)}, u32[]{:S(2)}) collective-permute-start(bf16[2,8,128,128]{3,2,1,0:T(8,128)(2,1)S(1)} %add_convert_fusion.2), channel_id=1, source_target_pairs={{0,4},{4,0},{8,12},{12,8},{1,5},{5,1},{9,13},{13,9},{2,6},{6,2},{1... | collective-permute-start | bytes 1572872 | tf_op jit(solution)/shard_map/ppermute | solution.py:476
  232.9 12.2 %collective-permute-done.20 = bf16[2,10,128,128]{3,2,1,0:T(8,128)(2,1)S(1)} collective-permute-done((bf16[2,10,128,128]{3,2,1,0:T(8,128)(2,1)S(1)}, bf16[2,10,128,128]{3,2,1,0:T(8,128)(2,1)S(1)}, u32[]{:S(2)}, u32[]{:S(2)}) %collective-permute-start.20) | collective-permute-done | bytes 655392 | tf_op jit(solution)/shard_map/ppermute | solution.py:476
  245.0 1.1 collective-permute-start.7
  246.2 11.5 %collective-permute-done.21 = bf16[2,10,128,128]{3,2,1,0:T(8,128)(2,1)S(1)} collective-permute-done((bf16[2,10,128,128]{3,2,1,0:T(8,128)(2,1)S(1)}, bf16[2,10,128,128]{3,2,1,0:T(8,128)(2,1)S(1)}, u32[]{:S(2)}, u32[]{:S(2)}) %collective-permute-start.21) | collective-permute-done | bytes 655392 | tf_op jit(solution)/shard_map/ppermute | solution.py:476
  257.8 3.9 %collective-permute-done.12 = bf16[2,8,128,128]{3,2,1,0:T(8,128)(2,1)S(1)} collective-permute-done((bf16[2,8,128,128]{3,2,1,0:T(8,128)(2,1)S(1)}, bf16[2,8,128,128]{3,2,1,0:T(8,128)(2,1)S(1)}, u32[]{:S(2)}, u32[]{:S(2)}) %collective-permute-start.12) | collective-permute-done | bytes 524320 | tf_op jit(solution)/shard_map/ppermute | solution.py:476
  264.2 1.8 fusion.4
  266.0 1.1 copy.52
  268.0 1.4 collective-permute-done.15
  269.4 1.4 fusion.5
  (141 shorter events, 22.3 us)
Async XLA Ops:
  114.1 2.3 collective-permute-start
  114.6 4.6 %collective-permute-start.1 = (bf16[2,8,128,128]{3,2,1,0:T(8,128)(2,1)}, bf16[2,8,128,128]{3,2,1,0:T(8,128)(2,1)}, u32[]{:S(2)}, u32[]{:S(2)}) collective-permute-start(bf16[2,8,128,128]{3,2,1,0:T(8,128)(2,1)} %get-tuple-element.56), channel_id=1, source_target_pairs={{0,1},{1,0},{2,3},{3,2},{4,5},{5,4},{6,7},{7,6},{8,9},{9,8},{10,11... | collective-permute-start | bytes 1572872 | tf_op jit(solution)/shard_map/ppermute | solution.py:476
  114.7 7.1 %collective-permute-start.2 = (bf16[2,8,128,128]{3,2,1,0:T(8,128)(2,1)}, bf16[2,8,128,128]{3,2,1,0:T(8,128)(2,1)}, u32[]{:S(2)}, u32[]{:S(2)}) collective-permute-start(bf16[2,8,128,128]{3,2,1,0:T(8,128)(2,1)} %get-tuple-element.58), channel_id=1, source_target_pairs={{0,1},{1,0},{2,3},{3,2},{4,5},{5,4},{6,7},{7,6},{8,9},{9,8},{10,11... | collective-permute-start | bytes 1572872 | tf_op jit(solution)/shard_map/ppermute | solution.py:476
  115.1 8.8 %collective-permute-start.3 = (bf16[2,8,128,128]{3,2,1,0:T(8,128)(2,1)}, bf16[2,8,128,128]{3,2,1,0:T(8,128)(2,1)}, u32[]{:S(2)}, u32[]{:S(2)}) collective-permute-start(bf16[2,8,128,128]{3,2,1,0:T(8,128)(2,1)} %get-tuple-element.60), channel_id=1, source_target_pairs={{0,1},{1,0},{2,3},{3,2},{4,5},{5,4},{6,7},{7,6},{8,9},{9,8},{10,11... | collective-permute-start | bytes 1572872 | tf_op jit(solution)/shard_map/ppermute | solution.py:476
  115.2 58.0 %collective-permute-start.22 = (bf16[2,10,128,128]{3,2,1,0:T(8,128)(2,1)}, bf16[2,10,128,128]{3,2,1,0:T(8,128)(2,1)S(1)}, u32[]{:S(2)}, u32[]{:S(2)}) collective-permute-start(bf16[2,10,128,128]{3,2,1,0:T(8,128)(2,1)} %get-tuple-element.88), channel_id=1, source_target_pairs={{0,1},{1,0},{2,3},{3,2},{4,5},{5,4},{6,7},{7,6},{8,9},{9,8},{10,11... | collective-permute-start | bytes 1966088 | tf_op jit(solution)/shard_map/ppermute | solution.py:476
  116.5 57.8 %collective-permute-start.23 = (bf16[2,10,128,128]{3,2,1,0:T(8,128)(2,1)}, bf16[2,10,128,128]{3,2,1,0:T(8,128)(2,1)}, u32[]{:S(2)}, u32[]{:S(2)}) collective-permute-start(bf16[2,10,128,128]{3,2,1,0:T(8,128)(2,1)} %get-tuple-element.89), channel_id=1, source_target_pairs={{0,2},{1,3},{2,0},{3,1},{4,6},{5,7},{6,4},{7,5},{8,10},{9,11},{10,... | collective-permute-start | bytes 1966088 | tf_op jit(solution)/shard_map/ppermute | solution.py:476
  119.1 56.6 %collective-permute-start.24 = (bf16[2,10,128,128]{3,2,1,0:T(8,128)(2,1)}, bf16[2,10,128,128]{3,2,1,0:T(8,128)(2,1)}, u32[]{:S(2)}, u32[]{:S(2)}) collective-permute-start(bf16[2,10,128,128]{3,2,1,0:T(8,128)(2,1)} %get-tuple-element.90), channel_id=1, source_target_pairs={{0,3},{1,2},{2,1},{3,0},{4,7},{5,6},{6,5},{7,4},{8,11},{9,10},{10,... | collective-permute-start | bytes 1966088 | tf_op jit(solution)/shard_map/ppermute | solution.py:476
  125.8 52.4 %collective-permute-start.6 = (bf16[2,8,128,128]{3,2,1,0:T(8,128)(2,1)}, bf16[2,8,128,128]{3,2,1,0:T(8,128)(2,1)}, u32[]{:S(2)}, u32[]{:S(2)}) collective-permute-start(bf16[2,8,128,128]{3,2,1,0:T(8,128)(2,1)} %add_convert_fusion.4), channel_id=1, source_target_pairs={{0,12},{4,8},{8,4},{12,0},{1,13},{5,9},{9,5},{13,1},{2,14},{6,10},... | collective-permute-start | bytes 1572872 | tf_op jit(solution)/shard_map/ppermute | solution.py:476
  171.0 6.2 %collective-permute-start.13 = (bf16[2,8,128,128]{3,2,1,0:T(8,128)(2,1)}, bf16[2,8,128,128]{3,2,1,0:T(8,128)(2,1)S(1)}, u32[]{:S(2)}, u32[]{:S(2)}) collective-permute-start(bf16[2,8,128,128]{3,2,1,0:T(8,128)(2,1)} %get-tuple-element.78), channel_id=1, source_target_pairs={{0,1},{1,0},{2,3},{3,2},{4,5},{5,4},{6,7},{7,6},{8,9},{9,8},{10,11... | collective-permute-start | bytes 1572872 | tf_op jit(solution)/shard_map/ppermute | solution.py:476
  173.3 4.5 %collective-permute-start.11 = (bf16[2,8,128,128]{3,2,1,0:T(8,128)(2,1)S(1)}, bf16[2,8,128,128]{3,2,1,0:T(8,128)(2,1)S(1)}, u32[]{:S(2)}, u32[]{:S(2)}) collective-permute-start(bf16[2,8,128,128]{3,2,1,0:T(8,128)(2,1)S(1)} %copy-done.30), channel_id=1, source_target_pairs={{0,1},{1,0},{2,3},{3,2},{4,5},{5,4},{6,7},{7,6},{8,9},{9,8},{10,11... | collective-permute-start | bytes 1572872 | tf_op jit(solution)/shard_map/ppermute | solution.py:476
  174.3 25.1 %copy-start.26 = (bf16[2,10,128,128]{3,2,1,0:T(8,128)(2,1)S(1)}, bf16[2,10,128,128]{3,2,1,0:T(8,128)(2,1)}, u32[]{:S(2)}) copy-start(bf16[2,10,128,128]{3,2,1,0:T(8,128)(2,1)} %get-tuple-element.81) | copy-start | bytes 1966084
  174.3 26.1 %copy-start.25 = (bf16[2,10,128,128]{3,2,1,0:T(8,128)(2,1)S(1)}, bf16[2,10,128,128]{3,2,1,0:T(8,128)(2,1)}, u32[]{:S(2)}) copy-start(bf16[2,10,128,128]{3,2,1,0:T(8,128)(2,1)} %get-tuple-element.82) | copy-start | bytes 1966084
  174.3 26.4 %copy-start.24 = (bf16[2,10,128,128]{3,2,1,0:T(8,128)(2,1)S(1)}, bf16[2,10,128,128]{3,2,1,0:T(8,128)(2,1)}, u32[]{:S(2)}) copy-start(bf16[2,10,128,128]{3,2,1,0:T(8,128)(2,1)} %get-tuple-element.84) | copy-start | bytes 1966084
  174.3 27.2 %copy-start.11 = (bf16[2,8,128,128]{3,2,1,0:T(8,128)(2,1)S(1)}, bf16[2,8,128,128]{3,2,1,0:T(8,128)(2,1)}, u32[]{:S(2)}) copy-start(bf16[2,8,128,128]{3,2,1,0:T(8,128)(2,1)} %get-tuple-element.73) | copy-start | bytes 1572868
  174.3 25.0 %collective-permute-start.5 = (bf16[2,8,128,128]{3,2,1,0:T(8,128)(2,1)S(1)}, bf16[2,8,128,128]{3,2,1,0:T(8,128)(2,1)S(1)}, u32[]{:S(2)}, u32[]{:S(2)}) collective-permute-start(bf16[2,8,128,128]{3,2,1,0:T(8,128)(2,1)S(1)} %copy-done.9), channel_id=1, source_target_pairs={{0,8},{4,12},{8,0},{12,4},{1,9},{5,13},{9,1},{13,5},{2,10},{6,14},... | collective-permute-start | bytes 1572872 | tf_op jit(solution)/shard_map/ppermute | solution.py:476
  175.8 24.6 %collective-permute-start.9 = (bf16[2,8,128,128]{3,2,1,0:T(8,128)(2,1)S(1)}, bf16[2,8,128,128]{3,2,1,0:T(8,128)(2,1)S(1)}, u32[]{:S(2)}, u32[]{:S(2)}) collective-permute-start(bf16[2,8,128,128]{3,2,1,0:T(8,128)(2,1)S(1)} %copy-done.29), channel_id=1, source_target_pairs={{0,1},{1,0},{2,3},{3,2},{4,5},{5,4},{6,7},{7,6},{8,9},{9,8},{10,11... | collective-permute-start | bytes 1572872 | tf_op jit(solution)/shard_map/ppermute | solution.py:476
  177.2 23.5 %collective-permute-start.8 = (bf16[2,8,128,128]{3,2,1,0:T(8,128)(2,1)S(1)}, bf16[2,8,128,128]{3,2,1,0:T(8,128)(2,1)S(1)}, u32[]{:S(2)}, u32[]{:S(2)}) collective-permute-start(bf16[2,8,128,128]{3,2,1,0:T(8,128)(2,1)S(1)} %copy-done.28), channel_id=1, source_target_pairs={{0,1},{1,0},{2,3},{3,2},{4,5},{5,4},{6,7},{7,6},{8,9},{9,8},{10,11... | collective-permute-start | bytes 1572872 | tf_op jit(solution)/shard_map/ppermute | solution.py:476
  177.8 25.8 %copy-start.23 = (bf16[2,10,128,128]{3,2,1,0:T(8,128)(2,1)S(1)}, bf16[2,10,128,128]{3,2,1,0:T(8,128)(2,1)}, u32[]{:S(2)}) copy-start(bf16[2,10,128,128]{3,2,1,0:T(8,128)(2,1)} %get-tuple-element.85) | copy-start | bytes 1966084
  177.8 26.9 %copy-start.22 = (bf16[2,10,128,128]{3,2,1,0:T(8,128)(2,1)S(1)}, bf16[2,10,128,128]{3,2,1,0:T(8,128)(2,1)}, u32[]{:S(2)}) copy-start(bf16[2,10,128,128]{3,2,1,0:T(8,128)(2,1)} %get-tuple-element.86) | copy-start | bytes 1966084
  177.8 26.9 %collective-permute-start.16 = (bf16[2,10,128,128]{3,2,1,0:T(8,128)(2,1)S(1)}, bf16[2,10,128,128]{3,2,1,0:T(8,128)(2,1)S(1)}, u32[]{:S(2)}, u32[]{:S(2)}) collective-permute-start(bf16[2,10,128,128]{3,2,1,0:T(8,128)(2,1)S(1)} %copy-done.27), channel_id=1, source_target_pairs={{0,1},{1,0},{2,3},{3,2},{4,5},{5,4},{6,7},{7,6},{8,9},{9,8},{10,11... | collective-permute-start | bytes 1966088 | tf_op jit(solution)/shard_map/ppermute | solution.py:476
  178.2 25.4 %collective-permute-start.4 = (bf16[2,8,128,128]{3,2,1,0:T(8,128)(2,1)S(1)}, bf16[2,8,128,128]{3,2,1,0:T(8,128)(2,1)S(1)}, u32[]{:S(2)}, u32[]{:S(2)}) collective-permute-start(bf16[2,8,128,128]{3,2,1,0:T(8,128)(2,1)S(1)} %copy-done.8), channel_id=1, source_target_pairs={{0,4},{4,0},{8,12},{12,8},{1,5},{5,1},{9,13},{13,9},{2,6},{6,2},{1... | collective-permute-start | bytes 1572872 | tf_op jit(solution)/shard_map/ppermute | solution.py:476
  199.3 17.6 %collective-permute-start.17 = (bf16[2,10,128,128]{3,2,1,0:T(8,128)(2,1)S(1)}, bf16[2,10,128,128]{3,2,1,0:T(8,128)(2,1)S(1)}, u32[]{:S(2)}, u32[]{:S(2)}) collective-permute-start(bf16[2,10,128,128]{3,2,1,0:T(8,128)(2,1)S(1)} %copy-done.26), channel_id=1, source_target_pairs={{0,2},{1,3},{2,0},{3,1},{4,6},{5,7},{6,4},{7,5},{8,10},{9,11},{10,... | collective-permute-start | bytes 1966088 | tf_op jit(solution)/shard_map/ppermute | solution.py:476
  200.4 29.2 %collective-permute-start.18 = (bf16[2,10,128,128]{3,2,1,0:T(8,128)(2,1)S(1)}, bf16[2,10,128,128]{3,2,1,0:T(8,128)(2,1)S(1)}, u32[]{:S(2)}, u32[]{:S(2)}) collective-permute-start(bf16[2,10,128,128]{3,2,1,0:T(8,128)(2,1)S(1)} %copy-done.25), channel_id=1, source_target_pairs={{0,3},{1,2},{2,1},{3,0},{4,7},{5,6},{6,5},{7,4},{8,11},{9,10},{10,... | collective-permute-start | bytes 1966088 | tf_op jit(solution)/shard_map/ppermute | solution.py:476
  200.7 28.9 %collective-permute-start.19 = (bf16[2,10,128,128]{3,2,1,0:T(8,128)(2,1)S(1)}, bf16[2,10,128,128]{3,2,1,0:T(8,128)(2,1)S(1)}, u32[]{:S(2)}, u32[]{:S(2)}) collective-permute-start(bf16[2,10,128,128]{3,2,1,0:T(8,128)(2,1)S(1)} %copy-done.24), channel_id=1, source_target_pairs={{0,1},{1,0},{2,3},{3,2},{4,5},{5,4},{6,7},{7,6},{8,9},{9,8},{10,11... | collective-permute-start | bytes 1966088 | tf_op jit(solution)/shard_map/ppermute | solution.py:476
  203.6 41.4 %collective-permute-start.20 = (bf16[2,10,128,128]{3,2,1,0:T(8,128)(2,1)S(1)}, bf16[2,10,128,128]{3,2,1,0:T(8,128)(2,1)S(1)}, u32[]{:S(2)}, u32[]{:S(2)}) collective-permute-start(bf16[2,10,128,128]{3,2,1,0:T(8,128)(2,1)S(1)} %copy-done.23), channel_id=1, source_target_pairs={{0,2},{1,3},{2,0},{3,1},{4,6},{5,7},{6,4},{7,5},{8,10},{9,11},{10,... | collective-permute-start | bytes 1966088 | tf_op jit(solution)/shard_map/ppermute | solution.py:476
  204.7 52.9 %collective-permute-start.21 = (bf16[2,10,128,128]{3,2,1,0:T(8,128)(2,1)S(1)}, bf16[2,10,128,128]{3,2,1,0:T(8,128)(2,1)S(1)}, u32[]{:S(2)}, u32[]{:S(2)}) collective-permute-start(bf16[2,10,128,128]{3,2,1,0:T(8,128)(2,1)S(1)} %copy-done.22), channel_id=1, source_target_pairs={{0,3},{1,2},{2,1},{3,0},{4,7},{5,6},{6,5},{7,4},{8,11},{9,10},{10,... | collective-permute-start | bytes 1966088 | tf_op jit(solution)/shard_map/ppermute | solution.py:476
  216.9 40.8 %collective-permute-start.14 = (bf16[2,8,128,128]{3,2,1,0:T(8,128)(2,1)S(1)}, bf16[2,8,128,128]{3,2,1,0:T(8,128)(2,1)S(1)}, u32[]{:S(2)}, u32[]{:S(2)}) collective-permute-start(bf16[2,8,128,128]{3,2,1,0:T(8,128)(2,1)S(1)} %add_convert_fusion), channel_id=1, source_target_pairs={{0,12},{4,8},{8,4},{12,0},{1,13},{5,9},{9,5},{13,1},{2,14},{6,10},... | collective-permute-start | bytes 1572872 | tf_op jit(solution)/shard_map/ppermute | solution.py:476
  229.5 32.2 %collective-permute-start.12 = (bf16[2,8,128,128]{3,2,1,0:T(8,128)(2,1)S(1)}, bf16[2,8,128,128]{3,2,1,0:T(8,128)(2,1)S(1)}, u32[]{:S(2)}, u32[]{:S(2)}) collective-permute-start(bf16[2,8,128,128]{3,2,1,0:T(8,128)(2,1)S(1)} %add_convert_fusion.1), channel_id=1, source_target_pairs={{0,8},{4,12},{8,0},{12,4},{1,9},{5,13},{9,1},{13,5},{2,10},{6,14},... | collective-permute-start | bytes 1572872 | tf_op jit(solution)/shard_map/ppermute | solution.py:476
  229.6 32.2 %collective-permute-start.10 = (bf16[2,8,128,128]{3,2,1,0:T(8,128)(2,1)S(1)}, bf16[2,8,128,128]{3,2,1,0:T(8,128)(2,1)S(1)}, u32[]{:S(2)}, u32[]{:S(2)}) collective-permute-start(bf16[2,8,128,128]{3,2,1,0:T(8,128)(2,1)S(1)} %add_convert_fusion.2), channel_id=1, source_target_pairs={{0,4},{4,0},{8,12},{12,8},{1,5},{5,1},{9,13},{13,9},{2,6},{6,2},{1... | collective-permute-start | bytes 1572872 | tf_op jit(solution)/shard_map/ppermute | solution.py:476
  232.7 30.0 %copy-start.4 = (bf16[2,40,128,128]{3,2,1,0:T(8,128)(2,1)}, bf16[2,40,128,128]{3,2,1,0:T(8,128)(2,1)S(1)}, u32[]{:S(2)}) copy-start(bf16[2,40,128,128]{3,2,1,0:T(8,128)(2,1)S(1)} %constant_dynamic-update-slice_fusion.14) | copy-start | bytes 7864324
  245.0 19.2 %collective-permute-start.7 = (bf16[8,128,128]{2,1,0:T(8,128)(2,1)S(1)}, bf16[8,128,128]{2,1,0:T(8,128)(2,1)S(1)}, u32[]{:S(2)}, u32[]{:S(2)}) collective-permute-start(bf16[8,128,128]{2,1,0:T(8,128)(2,1)S(1)} %fusion.2), channel_id=1, source_target_pairs={{0,2},{1,3},{2,0},{3,1},{4,6},{5,7},{6,4},{7,5},{8,10},{9,11},{10,... | collective-permute-start | bytes 786440 | tf_op jit(solution)/shard_map/ppermute | solution.py:476
  262.7 6.7 %collective-permute-start.15 = (bf16[8,128,128]{2,1,0:T(8,128)(2,1)}, bf16[8,128,128]{2,1,0:T(8,128)(2,1)}, u32[]{:S(2)}, u32[]{:S(2)}) collective-permute-start(bf16[8,128,128]{2,1,0:T(8,128)(2,1)} %fusion.3), channel_id=1, source_target_pairs={{0,2},{1,3},{2,0},{3,1},{4,6},{5,7},{6,4},{7,5},{8,10},{9,11},{10,... | collective-permute-start | bytes 786440 | tf_op jit(solution)/shard_map/ppermute | solution.py:476
  (24 other events, 139.2 us)
where the time goes:
time: 273 us; the launch traced here: 272 us
  Pallas kernels  145 us (53%)
  waiting for transfers between devices  71.9 us (26%)
  starting transfers between devices  19.8 us (7%)
  other arithmetic  17.3 us (6%)
  local copies, waits for them, and re-layouts  16.2 us (6%)
    pallas_call x1, Pallas kernels, gather(): pl.pallas_call(functools.partial(gather_kernel, shards), out_shape=[jax.S...  77.2 us
    ppermute x25, waiting for transfers between devices, swap(): lax.ppermute(value, axis, [(i, i ^ flip) for i in range(lax.axis_size(axi...  71.9 us
    pallas_call x3, Pallas kernels, columns(): pl.pallas_call(functools.partial(body, (slots, per_dev, tok, blk, shards)...  68.2 us
    ppermute x25, starting transfers between devices, swap(): lax.ppermute(value, axis, [(i, i ^ flip) for i in range(lax.axis_size(axi...  19.8 us
    convert_element_type x8, other arithmetic, chip_sum(): (a.astype(f32) + swap(b, 1).astype(f32)).astype(bf)  7.72 us
  transfers between devices with their start and end apart: 25, of which 10 were waited for; matrix products, arithmetic and copies ran while one was open for 7% of the time, Pallas kernels for 16%

commit v1 on v0

--- a/solution.py
+++ b/solution.py
@@ -307,9 +307,9 @@
 dot = functools.partial(lax.dot_general, preferred_element_type=jnp.float32)
 
 
-def load(rows_ref, tok_ref, tok, which, array, slot, sel):
+def load(rows_ref, tok_ref, tok, which, array, slot, r, sel):
     per_shard, blk = tok_ref.shape[4], tok_ref.shape[6]
-    place = rows_ref[array, slot, pl.program_id(0)]
+    place = rows_ref[array, slot, r]
     shard, block = place // per_shard, place % per_shard
     for c in range(2):
         for x in range(2):
@@ -317,11 +317,11 @@
             sel[q * tok : (q + 1) * tok, slot * blk : (slot + 1) * blk] = tok_ref[c, shard, x, which, block]
 
 
-def scaled(scale_ref, own, recv, array, slot):
+def scaled(scale_ref, own, recv, array, slot, r):
     per_dev = own.shape[0]
     src, sub = slot // per_dev, slot % per_dev
     value = recv[src - 1, sub, 0] if src else own[sub, 0]
-    return (value.astype(jnp.float32) * scale_ref[array, slot, pl.program_id(0)]).astype(jnp.bfloat16)
+    return (value.astype(jnp.float32) * scale_ref[array, slot, r]).astype(jnp.bfloat16)
 
 
 def accumulate(rows_ref, acc, array, slots, blk, product):
@@ -335,13 +335,13 @@
         acc[...] = jnp.zeros_like(acc)
 
 
-def flush(place_ref, acc, tok, own, other):
+def flush(shard, acc, tok, own, other):
     per_shard = own[0].shape[1]
 
     @pl.when(pl.program_id(0) == pl.num_programs(0) - 1)
     def _():
         for m in range(len(own)):
-            first = (place_ref[1] ^ m) * per_shard
+            first = (shard ^ m) * per_shard
             for c, ref in enumerate((own[m], other[m])):
                 for x in range(2):
                     q = c * 2 + x
@@ -362,12 +362,12 @@
     clear(acc)
     for slot in range(slots):
         span = slice(slot * blk, (slot + 1) * blk)
-        load(rows_ref, tok_ref, tok, 0, 0, slot, gate_sel)
-        load(rows_ref, tok_ref, tok, 0, 1, slot, up_sel)
-        load(rows_ref, tok_ref, tok, 1, 2, slot, down_sel)
-        gate_w[span, :] = scaled(scale_ref, own_w[0], recv_w[0], 0, slot)
-        up_w[span, :] = scaled(scale_ref, own_w[1], recv_w[1], 1, slot)
-        down_w[:, span] = scaled(scale_ref, own_w[2], recv_w[2], 2, slot)
+        load(rows_ref, tok_ref, tok, 0, 0, slot, r, gate_sel)
+        load(rows_ref, tok_ref, tok, 0, 1, slot, r, up_sel)
+        load(rows_ref, tok_ref, tok, 1, 2, slot, r, down_sel)
+        gate_w[span, :] = scaled(scale_ref, own_w[0], recv_w[0], 0, slot, r)
+        up_w[span, :] = scaled(scale_ref, own_w[1], recv_w[1], 1, slot, r)
+        down_w[:, span] = scaled(scale_ref, own_w[2], recv_w[2], 2, slot, r)
     gate_pre = dot(gate_sel[...], gate_w[...], NN)
     up_pre = dot(up_sel[...], up_w[...], NN)
     gate_pre_ref[0], up_pre_ref[0] = gate_pre, up_pre
@@ -378,20 +378,20 @@
         g = down[:, slot * blk : (slot + 1) * blk] * scale_ref[2, slot, r]
         grads[src][sub, 0] = g.astype(jnp.bfloat16)
     accumulate(rows_ref, acc, 2, slots, blk, dot(hidden, down_w[...], NN))
-    flush(place_ref, acc, tok, own, other)
-
-
-def middle_kernel(dims, rows_ref, scale_ref, place_ref, tok_ref, own_w, recv_w, gate_pre_ref, up_pre_ref, *refs):
+    flush(place_ref[1], acc, tok, own, other)
+
+
+def middle_kernel(dims, begin, rows_ref, scale_ref, place_ref, tok_ref, own_w, recv_w, gate_pre_ref, up_pre_ref, *refs):
     slots, per_dev, tok, blk, _ = dims
     nsrc = slots // per_dev
     grads, (gate_act_ref, up_act_ref), scratch = (refs[:nsrc], refs[nsrc : 2 * nsrc]), refs[2 * nsrc : 2 * nsrc + 2], refs[2 * nsrc + 2 :]
     gate_sel, up_sel, down_sel, down_w = scratch
-    r = pl.program_id(0)
+    r = pl.program_id(0) + begin
     for slot in range(slots):
-        load(rows_ref, tok_ref, tok, 0, 0, slot, gate_sel)
-        load(rows_ref, tok_ref, tok, 0, 1, slot, up_sel)
-        load(rows_ref, tok_ref, tok, 1, 2, slot, down_sel)
-        down_w[:, slot * blk : (slot + 1) * blk] = scaled(scale_ref, own_w, recv_w, 2, slot)
+        load(rows_ref, tok_ref, tok, 0, 0, slot, r, gate_sel)
+        load(rows_ref, tok_ref, tok, 0, 1, slot, r, up_sel)
+        load(rows_ref, tok_ref, tok, 1, 2, slot, r, down_sel)
+        down_w[:, slot * blk : (slot + 1) * blk] = scaled(scale_ref, own_w, recv_w, 2, slot, r)
     gate_pre, up_pre = gate_pre_ref[0], up_pre_ref[0]
     grad_hidden = dot(down_sel[...], down_w[...], NT)
     sig = jax.nn.sigmoid(gate_pre)
@@ -408,21 +408,30 @@
         grads[1][src][sub, 0] = g.astype(jnp.bfloat16)
 
 
-def late_kernel(dims, rows_ref, scale_ref, place_ref, *refs):
+def late_kernel(dims, splits, rows_ref, scale_ref, place_ref, *refs):
     slots, _, tok, blk, shards = dims
-    own_w, recv_w, (gate_act_ref, up_act_ref), refs = refs[:2], refs[2:4], refs[4:6], refs[6:]
-    own, other, (acc, gate_w, up_w) = refs[:shards], refs[shards : 2 * shards], refs[2 * shards :]
+    own_w, recv_w, refs = refs[:2], refs[2:4], refs[4:]
+    kept, refs = refs[: 2 * len(splits)], refs[2 * len(splits) :]
+    own_ref, other_ref, acc, gate_w, up_w = refs
+    own, other = [own_ref.at[d] for d in range(shards)], [other_ref.at[d] for d in range(shards)]
+    r = pl.program_id(0)
     clear(acc)
     for slot in range(slots):
         span = slice(slot * blk, (slot + 1) * blk)
-        gate_w[span, :] = scaled(scale_ref, own_w[0], recv_w[0], 0, slot)
-        up_w[span, :] = scaled(scale_ref, own_w[1], recv_w[1], 1, slot)
-    accumulate(rows_ref, acc, 0, slots, blk, dot(gate_act_ref[0], gate_w[...], NT))
-    accumulate(rows_ref, acc, 1, slots, blk, dot(up_act_ref[0], up_w[...], NT))
-    flush(place_ref, acc, tok, own, other)
-
-
-def columns(which, scalars, tok_all, own_w, recv_w, kept):
+        gate_w[span, :] = scaled(scale_ref, own_w[0], recv_w[0], 0, slot, r)
+        up_w[span, :] = scaled(scale_ref, own_w[1], recv_w[1], 1, slot, r)
+    for i, begin in enumerate(splits):
+        end = splits[i + 1] if i + 1 < len(splits) else pl.num_programs(0)
+
+        @pl.when(jnp.logical_and(r >= begin, r < end))
+        def _():
+            accumulate(rows_ref, acc, 0, slots, blk, dot(kept[2 * i][0], gate_w[...], NT))
+            accumulate(rows_ref, acc, 1, slots, blk, dot(kept[2 * i + 1][0], up_w[...], NT))
+
+    flush(0, acc, tok, own, other)
+
+
+def columns(which, scalars, tok_all, own_w, recv_w, kept, splits):
     nsrc = 1 + recv_w[0].shape[0]
     _, per_dev, count, blk, _ = recv_w[0].shape
     _, shards, _, _, per_shard, tok, _ = tok_all.shape
@@ -430,46 +439,234 @@
     slots = per_dev * nsrc
     total = 4 * tok
     bf, f32 = jnp.bfloat16, jnp.float32
+    ends = splits[1:] + (count,)
+    begin, steps = (splits[which], ends[which] - splits[which]) if isinstance(which, int) else (0, count)
     whole = lambda a: pl.BlockSpec(a, lambda r, *_: (0,) * len(a), pipeline_mode=pl.Buffered(1))
-    own_block = pl.BlockSpec((per_dev, 1, blk, blk), lambda r, rows, scale, at: (0, at[0] * count + r, 0, 0))
-    recv_block = pl.BlockSpec((nsrc - 1, per_dev, 1, blk, blk), lambda r, *_: (0, 0, r, 0, 0))
+    own_block = pl.BlockSpec((per_dev, 1, blk, blk), lambda r, rows, scale, at: (0, at[0] * count + begin + r, 0, 0))
+    recv_block = pl.BlockSpec((nsrc - 1, per_dev, 1, blk, blk), lambda r, *_: (0, 0, begin + r, 0, 0))
     block = pl.BlockSpec((per_dev, 1, blk, blk), lambda r, *_: (0, r, 0, 0))
-    piece = jax.ShapeDtypeStruct((per_dev, count, blk, blk), bf)
-    kept_block = [pl.BlockSpec((1, total, blk), lambda r, *_: (r, 0, 0))] * 2
-    keep = lambda kind: [jax.ShapeDtypeStruct((count, total, blk), kind)] * 2
-    sum_block = [whole((2, per_shard, tok, blk))] * (2 * shards)
-    sums = [jax.ShapeDtypeStruct((2, per_shard, tok, blk), bf)] * (2 * shards)
+    piece = jax.ShapeDtypeStruct((per_dev, steps, blk, blk), bf)
+    clipped = lambda low, size: pl.BlockSpec((1, total, blk), lambda r, *_: (jnp.clip(r - low, 0, size - 1), 0, 0))
+    keep = lambda kind: [jax.ShapeDtypeStruct((steps, total, blk), kind)] * 2
+    share = (2, per_shard, tok, blk)
     acc = pltpu.VMEM((nblk, total, blk), f32)
     sel = pltpu.VMEM((total, slots * blk), bf)
     tall, wide = pltpu.VMEM((slots * blk, blk), bf), pltpu.VMEM((blk, slots * blk), bf)
+    dims = (slots, per_dev, tok, blk, shards)
     if which == "early":
-        body, products = early_kernel, 4
+        body, products = functools.partial(early_kernel, dims), 4
         in_specs = [whole(tok_all.shape)] + [own_block] * 3 + [recv_block] * 3
         operands = (tok_all, *own_w, *recv_w)
-        out_specs, out_shape = [block] * nsrc + kept_block + sum_block, [piece] * nsrc + keep(f32) + sums
+        out_specs = [block] * nsrc + [clipped(0, count)] * 2 + [whole(share)] * (2 * shards)
+        out_shape = [piece] * nsrc + keep(f32) + [jax.ShapeDtypeStruct(share, bf)] * (2 * shards)
         scratch = [acc, sel, sel, sel, tall, tall, wide]
-    elif which == "middle":
-        body, products = middle_kernel, 3
-        in_specs = [whole(tok_all.shape), own_block, recv_block] + kept_block
+    elif which == "late":
+        body, products = functools.partial(late_kernel, dims, splits), 2
+        in_specs = [own_block] * 2 + [recv_block] * 2
+        for low, high in zip(splits, ends):
+            in_specs += [clipped(low, high - low)] * 2
+        operands = (*own_w[:2], *recv_w[:2], *kept)
+        out_specs, out_shape = [whole((shards,) + share)] * 2, [jax.ShapeDtypeStruct((shards,) + share, bf)] * 2
+        scratch = [acc, tall, tall]
+    else:
+        body, products = functools.partial(middle_kernel, dims, begin), 3
+        pre = pl.BlockSpec((1, total, blk), lambda r, *_: (begin + r, 0, 0))
+        in_specs = [whole(tok_all.shape), own_block, recv_block] + [pre] * 2
         operands = (tok_all, own_w[2], recv_w[2], *kept)
-        out_specs, out_shape = [block] * (2 * nsrc) + kept_block, [piece] * (2 * nsrc) + keep(bf)
+        out_specs, out_shape = [block] * (2 * nsrc) + [clipped(0, steps)] * 2, [piece] * (2 * nsrc) + keep(bf)
         scratch = [sel, sel, sel, wide]
-    else:
-        body, products = late_kernel, 2
-        in_specs = [own_block] * 2 + [recv_block] * 2 + kept_block
-        operands = (*own_w[:2], *recv_w[:2], *kept)
-        out_specs, out_shape = sum_block, sums
-        scratch = [acc, tall, tall]
-    flops = 2 * products * slots * count * total * blk * blk
+    flops = 2 * products * slots * steps * total * blk * blk
     return pl.pallas_call(
-        functools.partial(body, (slots, per_dev, tok, blk, shards)),
+        body,
         grid_spec=pltpu.PrefetchScalarGridSpec(
-            num_scalar_prefetch=3, grid=(count,), in_specs=in_specs, out_specs=out_specs, scratch_shapes=scratch,
+            num_scalar_prefetch=3, grid=(steps,), in_specs=in_specs, out_specs=out_specs, scratch_shapes=scratch,
         ),
         out_shape=out_shape,
         compiler_params=pltpu.CompilerParams(vmem_limit_bytes=60 * 1024 * 1024),
         cost_estimate=pl.CostEstimate(flops=flops, bytes_accessed=40 << 20, transcendentals=0),
     )(*scalars, *operands)
+
+
+def add_kernel(pairs, *refs):
+    for a, b, out in zip(refs[:pairs], refs[pairs : 2 * pairs], refs[2 * pairs :]):
+        out[...] = (a[...].astype(jnp.float32) + b[...].astype(jnp.float32)).astype(out.dtype)
+
+
+def add_pairs(left, right):
+    pairs, (near, blocks, tok, blk) = len(left), left[0].shape
+    spec = pl.BlockSpec((1, blocks // 2, tok, blk), lambda i, j: (i, j, 0, 0))
+    return pl.pallas_call(
+        functools.partial(add_kernel, pairs),
+        grid=(near, 2),
+        in_specs=[spec] * (2 * pairs),
+        out_specs=[spec] * pairs,
+        out_shape=[jax.ShapeDtypeStruct(left[0].shape, left[0].dtype)] * pairs,
+        compiler_params=pltpu.CompilerParams(vmem_limit_bytes=32 * 1024 * 1024),
+    )(*left, *right)
+
+
+def reduce_kernel(shards, own, other, first, *refs):
+    shares, refs = refs[: shards - 1], refs[shards - 1 :]
+    (out_ref, in_ref, chip, core_box, line_box, far, far_box, near, early,
+     load_sem, core_send, core_recv, line_send, line_recv, far_send, far_recv, early_sem) = refs
+    part, t, f = lax.axis_index("parts"), lax.axis_index("tensor"), lax.axis_index("fsdp")
+    last = shards - 1
+    f32, bf = jnp.float32, jnp.bfloat16
+    partner = (part, t, (f // 2) * 2 + 1 - f % 2)
+    across = (part, t, (f + 2) % 4)
+
+    def to(where, src, dst, send, recv):
+        return pltpu.make_async_remote_copy(
+            src_ref=src, dst_ref=dst, send_sem=send, recv_sem=recv,
+            device_id=where, device_id_type=pl.DeviceIdType.MESH,
+        )
+
+    barrier = pltpu.get_barrier_semaphore()
+    for where in (partner, across):
+        pl.semaphore_signal(barrier, inc=1, device_id=where, device_id_type=pl.DeviceIdType.MESH)
+
+    @pl.when(t > 0)
+    def _():
+        pl.semaphore_signal(barrier, inc=1, device_id=(part, t - 1, f), device_id_type=pl.DeviceIdType.MESH)
+
+    @pl.when(t < last)
+    def _():
+        pl.semaphore_signal(barrier, inc=1, device_id=(part, t + 1, f), device_id_type=pl.DeviceIdType.MESH)
+
+    ends = jnp.logical_or(t == 0, t == last)
+
+    @pl.when(ends)
+    def _():
+        pl.semaphore_wait(barrier, 3)
+
+    @pl.when(jnp.logical_not(ends))
+    def _():
+        pl.semaphore_wait(barrier, 4)
+
+    def place(i):
+        return jnp.where(t * 2 < shards, last - i, i)
+
+    order = [(i, x) for i in range(shards) for x in (1, 0)]
+    cores, loads = {}, {}
+    for i, x in order:
+        d = place(i)
+        cores[i, x] = to(partner, other.at[d, x], core_box.at[d, x], core_send.at[d, x], core_recv.at[d, x])
+        loads[i, x] = pltpu.make_async_copy(own.at[d, x], chip.at[d, x], load_sem.at[d, x])
+        cores[i, x].start()
+        loads[i, x].start()
+    fetch = [
+        pltpu.make_async_copy(ref, early.at[k], early_sem.at[k]) for k, ref in enumerate((first,) + tuple(shares))
+    ]
+    for c in fetch:
+        c.start()
+
+    def line(up, d, x):
+        where = (part, jnp.where(up, t + 1, t - 1), f)
+        w = jnp.where(up, 0, 1)
+        return to(where, chip.at[d, x], line_box.at[w, d, x], line_send.at[w, d, x], line_recv.at[w, d, x])
+
+    def gathered(i, x):
+        d = place(i)
+        loads[i, x].wait()
+        cores[i, x].wait_recv()
+        chip[d, x] = (chip[d, x].astype(f32) + core_box[d, x].astype(f32)).astype(bf)
+
+    def forward(up, i, x):
+        d = jnp.where(up, last - i, i)
+        w = jnp.where(up, 0, 1)
+        fed = jnp.where(up, t > 0, t < last)
+
+        @pl.when(jnp.where(up, t < d, t > d))
+        def _():
+            @pl.when(fed)
+            def _():
+                line(up, d, x).wait_recv()
+                chip[d, x] = (chip[d, x].astype(f32) + line_box[w, d, x].astype(f32)).astype(bf)
+
+            line(up, d, x).start()
+
+    low = t * 2 < shards
+    for i, x in order:
+        gathered(i, x)
+
+        @pl.when(jnp.where(low, t == 0, t == last))
+        def _():
+            forward(low, i, x)
+
+    for i in range(shards - 1):
+        for x in (1, 0):
+            @pl.when(jnp.logical_not(ends))
+            def _():
+                forward(low, i, x)
+
+        for x in (1, 0):
+            forward(jnp.logical_not(low), i, x)
+
+    def send_far(k):
+        return to(across, far.at[k], far_box.at[k], far_send.at[k], far_recv.at[k])
+
+    for c in fetch:
+        c.wait()
+
+    def early_sum(x):
+        return sum(early[k, x].astype(f32) for k in range(shards))
+
+    far[0] = early_sum(1).astype(bf)
+    send_far(0).start()
+    near[0] = early_sum(0)
+
+    def late_sum(x):
+        near[1] = chip[t, x].astype(f32)
+        for up in (True, False):
+            @pl.when(t > 0 if up else t < last)
+            def _():
+                line(jnp.bool_(up), t, x).wait_recv()
+                near[1] += line_box[0 if up else 1, t, x].astype(f32)
+
+    late_sum(1)
+    far[1] = near[1].astype(bf)
+    send_far(1).start()
+    late_sum(0)
+    blocks, blk = near.shape[1], near.shape[3]
+    for k, ref in enumerate((out_ref, in_ref)):
+        send_far(k).wait_recv()
+        for d in range(blocks):
+            ref[:, d * blk : (d + 1) * blk] = (near[k, d] + far_box[k, d].astype(f32)).astype(bf)
+    for k in range(2):
+        send_far(k).wait_send()
+    for i, x in order:
+        cores[i, x].wait_send()
+    for d in range(shards):
+        for x in range(2):
+            @pl.when(t < d)
+            def _():
+                line(jnp.bool_(True), d, x).wait_send()
+
+            @pl.when(t > d)
+            def _():
+                line(jnp.bool_(False), d, x).wait_send()
+
+
+def reduce(own, other, shares, width):
+    shards, _, blocks, tok, blk = own.shape
+    bf, f32 = jnp.bfloat16, jnp.float32
+    dma = lambda *a: pltpu.SemaphoreType.DMA(a)
+    anywhere = pl.BlockSpec(memory_space=pl.ANY)
+    unit = (blocks, tok, blk)
+    pair = (shards, 2)
+    return pl.pallas_call(
+        functools.partial(reduce_kernel, shards),
+        out_shape=[jax.ShapeDtypeStruct((tok, width), bf)] * 2,
+        in_specs=[anywhere] * (2 + shards),
+        out_specs=[pl.BlockSpec(memory_space=pltpu.VMEM)] * 2,
+        scratch_shapes=[
+            pltpu.VMEM(pair + unit, bf), pltpu.VMEM(pair + unit, bf), pltpu.VMEM((2,) + pair + unit, bf),
+            pltpu.VMEM((2,) + unit, bf), pltpu.VMEM((2,) + unit, bf), pltpu.VMEM((2,) + unit, f32),
+            pltpu.VMEM(pair + unit, bf),
+            dma(*pair), dma(*pair), dma(*pair), dma(2, *pair), dma(2, *pair), dma(2), dma(2), dma(shards),
+        ],
+        compiler_params=pltpu.CompilerParams(collective_id=1, has_side_effects=True, vmem_limit_bytes=24 * 1024 * 1024),
+    )(own, other, *shares)
 
 
 def swap(value, flip, axis="fsdp"):
@@ -507,40 +704,35 @@
     table = jnp.concatenate([kept, table]).transpose(1, 0, 2, 3).reshape(6, 4 * per_dev, count)
     table_rows = table[:3].astype(jnp.int32)
     table_scale = table[3:]
-
-    def home(pieces):
+    splits = (0, (count + 1) // 2)
+
+    def home(parts):
         result = jnp.zeros((per_dev, local_cols, blk, blk), bf)
-        for m, part in enumerate(pieces):
-            result = lax.dynamic_update_slice_in_dim(result, part, (mine ^ m) * count, axis=1)
+        for begin, pieces in parts:
+            for m, piece in enumerate(pieces):
+                result = lax.dynamic_update_slice_in_dim(result, piece, (mine ^ m) * count + begin, axis=1)
         return result
 
     def send(pieces):
         return [p if m == 0 else swap(p, m) for m, p in enumerate(pieces)]
 
-    def chip_sum(own, other):
-        return [(a.astype(f32) + swap(b, 1).astype(f32)).astype(bf) for a, b in zip(own, other)]
-
-    def scatter(chip):
-        return [c if m == 0 else swap(c, m, "tensor") for m, c in enumerate(chip)]
-
-    def finish(shares):
-        far = sum(s[1].astype(f32) for s in shares).astype(bf)
-        total = (sum(s[0].astype(f32) for s in shares) + swap(far, 2).astype(f32)).astype(bf)
-        return total.transpose(1, 0, 2).reshape(tok, width)
-
     scalars = (table_rows, table_scale, jnp.stack([mine, shard]).astype(jnp.int32))
-    early = columns("early", scalars, tok_all, own_w, recv_w, ())
+    early = columns("early", scalars, tok_all, own_w, recv_w, (), splits)
     down_pieces, pre, own, other = early[:4], early[4:6], early[6 : 6 + shards], early[6 + shards :]
-    chip = chip_sum(own, other)
+    chip = add_pairs(own, [swap(b, 1) for b in other])
     down_sent = send(down_pieces)
     chip, pre = lax.optimization_barrier((chip, pre))
-    out_shares = scatter(chip)
-    middle = columns("middle", scalars, tok_all, own_w, recv_w, pre)
-    gate_sent, up_sent = send(middle[:4]), send(middle[4:8])
-    late = columns("late", scalars, tok_all, own_w, recv_w, middle[8:])
-    chip = chip_sum(late[:shards], late[shards:])
-    in_shares = scatter(chip)
-    return (finish(out_shares), finish(in_shares), home(gate_sent), home(up_sent), home(down_sent))
+    out_shares = [c if m == 0 else swap(c, m, "tensor") for m, c in enumerate(chip)]
+    acts, gate_sent, up_sent = [], [], []
+    for i, begin in enumerate(splits):
+        middle = columns(i, scalars, tok_all, own_w, recv_w, pre, splits)
+        gate_sent.append((begin, send(middle[:4])))
+        up_sent.append((begin, send(middle[4:8])))
+        acts += middle[8:]
+        pre, acts = lax.optimization_barrier((pre, acts))
+    own, other = columns("late", scalars, tok_all, own_w, recv_w, acts, splits)
+    layer_out, grad_tokens = reduce(own, other, out_shares, width)
+    return (layer_out, grad_tokens, home(gate_sent), home(up_sent), home([(0, down_sent)]))
 
 
 def choose_plan(mesh, *args):

time: 273 us -> 303 us (1.11)
  Pallas kernels: 145 us -> 203 us
  waiting for transfers between devices: 71.9 us -> 41.8 us
  local copies, waits for them, and re-layouts: 16.2 us -> 34.6 us
  other arithmetic: 17.3 us -> 4.3 us
  starting transfers between devices: 19.8 us -> 15.9 us
    pallas_call x3 -> x6, Pallas kernels: 68.2 us -> 125 us  [the longest x4 74.8 us: columns(): pl.pallas_call(body, grid_spec=pltpu.PrefetchScalarGridSpec(num_scalar_pr...]
    ppermute x25 -> x22, waiting for transfers between devices: 71.9 us -> 41.8 us  [swap(): lax.ppermute(value, axis, [(i, i ^ flip) for i in range(lax.axis_size(axi...]
    dynamic_update_slice x12 -> x19, local copies, waits for them, and re-layouts: 3.48 us -> 19.5 us  [home(): lax.dynamic_update_slice_in_dim(result, piece, (mine ^ m) * count + begin...]
    convert_element_type x8 -> x0, other arithmetic: 7.72 us -> none  [chip_sum(): (a.astype(f32) + swap(b, 1).astype(f32)).astype(bf)]
    ppermute x25 -> x22, starting transfers between devices: 19.8 us -> 15.9 us  [swap(): lax.ppermute(value, axis, [(i, i ^ flip) for i in range(lax.axis_size(axi...]
    transpose x2 -> x0, other arithmetic: 3.2 us -> none  [finish(): return total.transpose(1, 0, 2).reshape(tok, width)]
    unnamed x71 -> x67, local copies, waits for them, and re-layouts: 5.45 us -> 6.21 us
  transfers between devices with their start and end apart: 25 -> 22, of which waited for: 10 -> 8; matrix products, arithmetic and copies ran while one was open for 7% -> 8% of each run, Pallas kernels for 16% -> 17%
where the time goes in v1:
time: 303 us; the launch traced here: 300 us
  Pallas kernels  203 us (67%)
  waiting for transfers between devices  41.8 us (14%)
  local copies, waits for them, and re-layouts  34.6 us (11%)
  starting transfers between devices  15.9 us (5%)
  other arithmetic  4.3 us (1%)
    pallas_call x1, Pallas kernels, gather(): pl.pallas_call(functools.partial(gather_kernel, shards), out_shape=[jax.S...  77.2 us
    pallas_call x4, Pallas kernels, columns(): pl.pallas_call(body, grid_spec=pltpu.PrefetchScalarGridSpec(num_scalar_pr...  74.8 us
    pallas_call x1, Pallas kernels, reduce(): pl.pallas_call(functools.partial(reduce_kernel, shards), out_shape=[jax.S...  48.1 us
    ppermute x22, waiting for transfers between devices, swap(): lax.ppermute(value, axis, [(i, i ^ flip) for i in range(lax.axis_size(axi...  41.8 us
    dynamic_update_slice x19, local copies, waits for them, and re-layouts, home(): lax.dynamic_update_slice_in_dim(result, piece, (mine ^ m) * count + begin...  19.5 us
    ppermute x22, starting transfers between devices, swap(): lax.ppermute(value, axis, [(i, i ^ flip) for i in range(lax.axis_size(axi...  15.9 us
    unnamed x67, local copies, waits for them, and re-layouts  6.21 us
  transfers between devices with their start and end apart: 22, of which 8 were waited for; matrix products, arithmetic and copies ran while one was open for 8% of the time, Pallas kernels for 17%

profile of v1, /device:TPU:0, one launch (start us, length us, event | category | flops | bytes accessed | tf_op | source)
XLA Modules:
  0.0 300.3 jit_solution(7776293827021038820)
XLA Ops:
  5.2 1.1 copy.43
  6.5 1.1 copy.42
  7.9 0.8 maximum_bitcast_fusion.both
  8.7 77.2 %shard_map.146 = (bf16[2,4,2,2,8,128,128]{6,5,4,3,2,1,0:T(8,128)(2,1)}, bf16[3,2,10,128,128]{4,3,2,1,0:T(8,128)(2,1)}, bf16[3,2,10,128,128]{4,3,2,1,0:T(8,128)(2...) custom-call(f32[4,6,2,10]{3,2,1,0:T(2,128)} %bitcast.23, bf16[2,8,128,128]{3,2,1,0:T(8,128)(2,1)} %maximum_bitcast_fusion.both, ...), custom_call_target="tpu_custom_call" | custom-call | tf_op jit(solution)/shard_map/pallas_call | solution.py:291
  88.6 25.6 %shard_map.147 = (bf16[2,10,128,128]{3,2,1,0:T(8,128)(2,1)}, bf16[2,10,128,128]{3,2,1,0:T(8,128)(2,1)}, bf16[2,10,128,128]{3,2,1,0:T(8,128)(2,1)}, bf16[2,10,128...) custom-call(s32[3,8,10]{2,1,0:T(8,128)} %bitcast.15, ...), custom_call_target="tpu_custom_call" | custom-call | flops 5368709120 | bytes 41943040 | tf_op jit(solution)/shard_map/pallas_call | solution.py:479
  116.3 1.2 constant_dynamic-update-slice_fusion.9
  117.6 1.6 collective-permute-start.20
  119.2 2.4 shard_map.148
  122.4 0.8 copy-done.8
  124.0 16.1 %shard_map.149 = (bf16[2,5,128,128]{3,2,1,0:T(8,128)(2,1)}, bf16[2,5,128,128]{3,2,1,0:T(8,128)(2,1)}, bf16[2,5,128,128]{3,2,1,0:T(8,128)(2,1)}, bf16[2,5,128,128...) custom-call(s32[3,8,10]{2,1,0:T(8,128)} %bitcast.16, ...), custom_call_target="tpu_custom_call" | custom-call | flops 2013265920 | bytes 41943040 | tf_op jit(solution)/shard_map/pallas_call | solution.py:479
  141.0 16.1 %shard_map.150 = (bf16[2,5,128,128]{3,2,1,0:T(8,128)(2,1)}, bf16[2,5,128,128]{3,2,1,0:T(8,128)(2,1)}, bf16[2,5,128,128]{3,2,1,0:T(8,128)(2,1)}, bf16[2,5,128,128...) custom-call(s32[3,8,10]{2,1,0:T(8,128)} %bitcast.17, ...), custom_call_target="tpu_custom_call" | custom-call | flops 2013265920 | bytes 41943040 | tf_op jit(solution)/shard_map/pallas_call | solution.py:479
  157.1 2.1 broadcast.3.clone
  160.0 2.1 broadcast.3.clone.1
  162.9 17.0 %shard_map.151 = (bf16[4,2,8,128,128]{4,3,2,1,0:T(8,128)(2,1)}, bf16[4,2,8,128,128]{4,3,2,1,0:T(8,128)(2,1)}) custom-call(s32[3,8,10]{2,1,0:T(8,128)} %bitcast.18, f32[3,8,10]{2,1,0:T(8,128)} %bitcast.22, s32[2]{0:T(128)} %pad_add_fusion.place_ref, bf16[2,40,128,128]{3,2,1,0:T(8,128)(2,1)} %refs_0_.3, bf16[2,40,128,128]{3,2,1,0:T(8,128)(2,1)} %refs_1_.3, ...), custom_call_target="tpu_custom_call" | custom-call | flops 2684354560 | bytes 41943040 | tf_op jit(solution)/shard_map/pallas_call | solution.py:479
  180.0 1.6 collective-permute-start.14
  181.5 2.1 constant_dynamic-update-slice_fusion.8
  183.7 2.1 constant_dynamic-update-slice_fusion.7
  186.5 2.1 constant_dynamic-update-slice_fusion.6
  188.6 1.6 collective-permute-start.8
  191.8 4.8 %collective-permute-done.15 = bf16[2,5,128,128]{3,2,1,0:T(8,128)(2,1)S(1)} collective-permute-done((bf16[2,5,128,128]{3,2,1,0:T(8,128)(2,1)S(1)}, bf16[2,5,128,128]{3,2,1,0:T(8,128)(2,1)S(1)}, u32[]{:S(2)}, u32[]{:S(2)}) %collective-permute-start.15) | collective-permute-done | bytes 327712 | tf_op jit(solution)/shard_map/ppermute | solution.py:673
  198.2 1.5 collective-permute-start.11
  200.5 4.1 %collective-permute-done.8 = bf16[2,5,128,128]{3,2,1,0:T(8,128)(2,1)S(1)} collective-permute-done((bf16[2,5,128,128]{3,2,1,0:T(8,128)(2,1)S(1)}, bf16[2,5,128,128]{3,2,1,0:T(8,128)(2,1)S(1)}, u32[]{:S(2)}, u32[]{:S(2)}) %collective-permute-start.8) | collective-permute-done | bytes 327712 | tf_op jit(solution)/shard_map/ppermute | solution.py:673
  205.4 5.2 %collective-permute-done.9 = bf16[2,5,128,128]{3,2,1,0:T(8,128)(2,1)S(1)} collective-permute-done((bf16[2,5,128,128]{3,2,1,0:T(8,128)(2,1)S(1)}, bf16[2,5,128,128]{3,2,1,0:T(8,128)(2,1)S(1)}, u32[]{:S(2)}, u32[]{:S(2)}) %collective-permute-start.9) | collective-permute-done | bytes 327712 | tf_op jit(solution)/shard_map/ppermute | solution.py:673
  212.1 1.0 constant_dynamic-update-slice_fusion.13
  213.1 2.9 collective-permute-start.5
  216.7 2.0 collective-permute-done.11
  218.7 2.5 collective-permute-start.6
  222.0 3.4 %collective-permute-done.17 = bf16[2,5,128,128]{3,2,1,0:T(8,128)(2,1)S(1)} collective-permute-done((bf16[2,5,128,128]{3,2,1,0:T(8,128)(2,1)S(1)}, bf16[2,5,128,128]{3,2,1,0:T(8,128)(2,1)S(1)}, u32[]{:S(2)}, u32[]{:S(2)}) %collective-permute-start.17) | collective-permute-done | bytes 327712 | tf_op jit(solution)/shard_map/ppermute | solution.py:673
  226.9 4.5 %collective-permute-done.12 = bf16[2,5,128,128]{3,2,1,0:T(8,128)(2,1)S(1)} collective-permute-done((bf16[2,5,128,128]{3,2,1,0:T(8,128)(2,1)S(1)}, bf16[2,5,128,128]{3,2,1,0:T(8,128)(2,1)S(1)}, u32[]{:S(2)}, u32[]{:S(2)}) %collective-permute-start.12) | collective-permute-done | bytes 327712 | tf_op jit(solution)/shard_map/ppermute | solution.py:673
  232.2 6.0 %collective-permute-done.18 = bf16[2,5,128,128]{3,2,1,0:T(8,128)(2,1)S(1)} collective-permute-done((bf16[2,5,128,128]{3,2,1,0:T(8,128)(2,1)S(1)}, bf16[2,5,128,128]{3,2,1,0:T(8,128)(2,1)S(1)}, u32[]{:S(2)}, u32[]{:S(2)}) %collective-permute-start.18) | collective-permute-done | bytes 327712 | tf_op jit(solution)/shard_map/ppermute | solution.py:673
  239.0 11.8 %collective-permute-done.5.refs_1_ = bf16[2,8,128,128]{3,2,1,0:T(8,128)(2,1)S(1)} collective-permute-done((bf16[2,8,128,128]{3,2,1,0:T(8,128)(2,1)S(1)}, bf16[2,8,128,128]{3,2,1,0:T(8,128)(2,1)S(1)}, u32[]{:S(2)}, u32[]{:S(2)}) %collective-permute-start.5) | collective-permute-done | bytes 524320 | tf_op jit(solution)/shard_map/ppermute | solution.py:673
  250.8 48.1 %shard_map.152 = (bf16[128,1024]{1,0:T(8,128)(2,1)S(1)}, bf16[128,1024]{1,0:T(8,128)(2,1)S(1)}) custom-call(bf16[4,2,8,128,128]{4,3,2,1,0:T(8,128)(2,1)S(1)} %copy-done, bf16[4,2,8,128,128]{4,3,2,1,0:T(8,128)(2,1)S(1)} %copy-done.1, bf16[2,8,128,128]{3,2,1,0:T(8,128)(2,1)S(1)} %get-tuple-element.101.first, ...), custom_call_target="tpu_custom_call" | custom-call | tf_op jit(solution)/shard_map/pallas_call | solution.py:657
  (127 shorter events, 26.7 us)
Async XLA Ops:
  114.2 3.3 %collective-permute-start = (bf16[2,8,128,128]{3,2,1,0:T(8,128)(2,1)}, bf16[2,8,128,128]{3,2,1,0:T(8,128)(2,1)S(1)}, u32[]{:S(2)}, u32[]{:S(2)}) collective-permute-start(bf16[2,8,128,128]{3,2,1,0:T(8,128)(2,1)} %get-tuple-element.75), channel_id=1, source_target_pairs={{0,1},{1,0},{2,3},{3,2},{4,5},{5,4},{6,7},{7,6},{8,9},{9,8},{10,11... | collective-permute-start | bytes 1572872 | tf_op jit(solution)/shard_map/ppermute | solution.py:673
  114.7 4.4 %collective-permute-start.1 = (bf16[2,8,128,128]{3,2,1,0:T(8,128)(2,1)}, bf16[2,8,128,128]{3,2,1,0:T(8,128)(2,1)S(1)}, u32[]{:S(2)}, u32[]{:S(2)}) collective-permute-start(bf16[2,8,128,128]{3,2,1,0:T(8,128)(2,1)} %get-tuple-element.76), channel_id=1, source_target_pairs={{0,1},{1,0},{2,3},{3,2},{4,5},{5,4},{6,7},{7,6},{8,9},{9,8},{10,11... | collective-permute-start | bytes 1572872 | tf_op jit(solution)/shard_map/ppermute | solution.py:673
  114.8 4.3 %collective-permute-start.2 = (bf16[2,8,128,128]{3,2,1,0:T(8,128)(2,1)}, bf16[2,8,128,128]{3,2,1,0:T(8,128)(2,1)}, u32[]{:S(2)}, u32[]{:S(2)}) collective-permute-start(bf16[2,8,128,128]{3,2,1,0:T(8,128)(2,1)} %get-tuple-element.77), channel_id=1, source_target_pairs={{0,1},{1,0},{2,3},{3,2},{4,5},{5,4},{6,7},{7,6},{8,9},{9,8},{10,11... | collective-permute-start | bytes 1572872 | tf_op jit(solution)/shard_map/ppermute | solution.py:673
  115.2 3.9 %collective-permute-start.3 = (bf16[2,8,128,128]{3,2,1,0:T(8,128)(2,1)}, bf16[2,8,128,128]{3,2,1,0:T(8,128)(2,1)}, u32[]{:S(2)}, u32[]{:S(2)}) collective-permute-start(bf16[2,8,128,128]{3,2,1,0:T(8,128)(2,1)} %get-tuple-element.78), channel_id=1, source_target_pairs={{0,1},{1,0},{2,3},{3,2},{4,5},{5,4},{6,7},{7,6},{8,9},{9,8},{10,11... | collective-permute-start | bytes 1572872 | tf_op jit(solution)/shard_map/ppermute | solution.py:673
  115.3 64.6 %collective-permute-start.19 = (bf16[2,10,128,128]{3,2,1,0:T(8,128)(2,1)}, bf16[2,10,128,128]{3,2,1,0:T(8,128)(2,1)}, u32[]{:S(2)}, u32[]{:S(2)}) collective-permute-start(bf16[2,10,128,128]{3,2,1,0:T(8,128)(2,1)} %get-tuple-element.124), channel_id=1, source_target_pairs={{0,1},{1,0},{2,3},{3,2},{4,5},{5,4},{6,7},{7,6},{8,9},{9,8},{10,11... | collective-permute-start | bytes 1966088 | tf_op jit(solution)/shard_map/ppermute | solution.py:673
  117.6 66.1 %collective-permute-start.20 = (bf16[2,10,128,128]{3,2,1,0:T(8,128)(2,1)}, bf16[2,10,128,128]{3,2,1,0:T(8,128)(2,1)}, u32[]{:S(2)}, u32[]{:S(2)}) collective-permute-start(bf16[2,10,128,128]{3,2,1,0:T(8,128)(2,1)} %get-tuple-element.125), channel_id=1, source_target_pairs={{0,2},{1,3},{2,0},{3,1},{4,6},{5,7},{6,4},{7,5},{8,10},{9,11},{10,... | collective-permute-start | bytes 1966088 | tf_op jit(solution)/shard_map/ppermute | solution.py:673
  119.1 66.7 %collective-permute-start.21 = (bf16[2,10,128,128]{3,2,1,0:T(8,128)(2,1)}, bf16[2,10,128,128]{3,2,1,0:T(8,128)(2,1)}, u32[]{:S(2)}, u32[]{:S(2)}) collective-permute-start(bf16[2,10,128,128]{3,2,1,0:T(8,128)(2,1)} %get-tuple-element.126), channel_id=1, source_target_pairs={{0,3},{1,2},{2,1},{3,0},{4,7},{5,6},{6,5},{7,4},{8,11},{9,10},{10,... | collective-permute-start | bytes 1966088 | tf_op jit(solution)/shard_map/ppermute | solution.py:673
  140.2 98.8 %collective-permute-start.4 = (bf16[2,8,128,128]{3,2,1,0:T(8,128)(2,1)S(1)}, bf16[2,8,128,128]{3,2,1,0:T(8,128)(2,1)S(1)}, u32[]{:S(2)}, u32[]{:S(2)}) collective-permute-start(bf16[2,8,128,128]{3,2,1,0:T(8,128)(2,1)S(1)} %copy-done.11), channel_id=1, source_target_pairs={{0,4},{4,0},{8,12},{12,8},{1,5},{5,1},{9,13},{13,9},{2,6},{6,2},{1... | collective-permute-start | bytes 1572872 | tf_op jit(solution)/shard_map/ppermute | solution.py:673
  140.3 48.3 %collective-permute-start.13 = (bf16[2,5,128,128]{3,2,1,0:T(8,128)(2,1)}, bf16[2,5,128,128]{3,2,1,0:T(8,128)(2,1)S(1)}, u32[]{:S(2)}, u32[]{:S(2)}) collective-permute-start(bf16[2,5,128,128]{3,2,1,0:T(8,128)(2,1)} %get-tuple-element.116), channel_id=1, source_target_pairs={{0,1},{1,0},{2,3},{3,2},{4,5},{5,4},{6,7},{7,6},{8,9},{9,8},{10,11... | collective-permute-start | bytes 983048 | tf_op jit(solution)/shard_map/ppermute | solution.py:673
  180.0 11.0 %collective-permute-start.14 = (bf16[2,5,128,128]{3,2,1,0:T(8,128)(2,1)S(1)}, bf16[2,5,128,128]{3,2,1,0:T(8,128)(2,1)S(1)}, u32[]{:S(2)}, u32[]{:S(2)}) collective-permute-start(bf16[2,5,128,128]{3,2,1,0:T(8,128)(2,1)S(1)} %copy-done.28), channel_id=1, source_target_pairs={{0,2},{1,3},{2,0},{3,1},{4,6},{5,7},{6,4},{7,5},{8,10},{9,11},{10,... | collective-permute-start | bytes 983048 | tf_op jit(solution)/shard_map/ppermute | solution.py:673
  183.6 21.0 %copy-start.21 = (bf16[2,5,128,128]{3,2,1,0:T(8,128)(2,1)S(1)}, bf16[2,5,128,128]{3,2,1,0:T(8,128)(2,1)}, u32[]{:S(2)}) copy-start(bf16[2,5,128,128]{3,2,1,0:T(8,128)(2,1)} %get-tuple-element.120) | copy-start | bytes 983044
  183.6 13.0 %collective-permute-start.15 = (bf16[2,5,128,128]{3,2,1,0:T(8,128)(2,1)S(1)}, bf16[2,5,128,128]{3,2,1,0:T(8,128)(2,1)S(1)}, u32[]{:S(2)}, u32[]{:S(2)}) collective-permute-start(bf16[2,5,128,128]{3,2,1,0:T(8,128)(2,1)S(1)} %copy-done.27), channel_id=1, source_target_pairs={{0,3},{1,2},{2,1},{3,0},{4,7},{5,6},{6,5},{7,4},{8,11},{9,10},{10,... | collective-permute-start | bytes 983048 | tf_op jit(solution)/shard_map/ppermute | solution.py:673
  185.9 24.8 %copy-start.20 = (bf16[2,5,128,128]{3,2,1,0:T(8,128)(2,1)S(1)}, bf16[2,5,128,128]{3,2,1,0:T(8,128)(2,1)}, u32[]{:S(2)}) copy-start(bf16[2,5,128,128]{3,2,1,0:T(8,128)(2,1)} %get-tuple-element.121) | copy-start | bytes 983044
  185.9 26.2 %copy-start.15 = (bf16[2,5,128,128]{3,2,1,0:T(8,128)(2,1)S(1)}, bf16[2,5,128,128]{3,2,1,0:T(8,128)(2,1)}, u32[]{:S(2)}) copy-start(bf16[2,5,128,128]{3,2,1,0:T(8,128)(2,1)} %get-tuple-element.111) | copy-start | bytes 983044
  185.9 26.2 %copy-start.16 = (bf16[2,5,128,128]{3,2,1,0:T(8,128)(2,1)S(1)}, bf16[2,5,128,128]{3,2,1,0:T(8,128)(2,1)}, u32[]{:S(2)}) copy-start(bf16[2,5,128,128]{3,2,1,0:T(8,128)(2,1)} %get-tuple-element.119) | copy-start | bytes 983044
  185.9 12.4 %collective-permute-start.7 = (bf16[2,5,128,128]{3,2,1,0:T(8,128)(2,1)S(1)}, bf16[2,5,128,128]{3,2,1,0:T(8,128)(2,1)S(1)}, u32[]{:S(2)}, u32[]{:S(2)}) collective-permute-start(bf16[2,5,128,128]{3,2,1,0:T(8,128)(2,1)S(1)} %copy-done.26), channel_id=1, source_target_pairs={{0,1},{1,0},{2,3},{3,2},{4,5},{5,4},{6,7},{7,6},{8,9},{9,8},{10,11... | collective-permute-start | bytes 983048 | tf_op jit(solution)/shard_map/ppermute | solution.py:673
  188.6 24.5 %copy-start.9 = (bf16[2,8,128,128]{3,2,1,0:T(8,128)(2,1)S(1)}, bf16[2,8,128,128]{3,2,1,0:T(8,128)(2,1)}, u32[]{:S(2)}) copy-start(bf16[2,8,128,128]{3,2,1,0:T(8,128)(2,1)} %copy-done.8) | copy-start | bytes 1572868
  188.6 16.0 %collective-permute-start.8 = (bf16[2,5,128,128]{3,2,1,0:T(8,128)(2,1)S(1)}, bf16[2,5,128,128]{3,2,1,0:T(8,128)(2,1)S(1)}, u32[]{:S(2)}, u32[]{:S(2)}) collective-permute-start(bf16[2,5,128,128]{3,2,1,0:T(8,128)(2,1)S(1)} %copy-done.25), channel_id=1, source_target_pairs={{0,2},{1,3},{2,0},{3,1},{4,6},{5,7},{6,4},{7,5},{8,10},{9,11},{10,... | collective-permute-start | bytes 983048 | tf_op jit(solution)/shard_map/ppermute | solution.py:673
  191.0 27.7 %copy-start.7 = (bf16[2,8,128,128]{3,2,1,0:T(8,128)(2,1)S(1)}, bf16[2,8,128,128]{3,2,1,0:T(8,128)(2,1)}, u32[]{:S(2)}) copy-start(bf16[2,8,128,128]{3,2,1,0:T(8,128)(2,1)} %copy-done.6) | copy-start | bytes 1572868
  191.0 30.2 %copy-start.19 = (bf16[2,5,128,128]{3,2,1,0:T(8,128)(2,1)S(1)}, bf16[2,5,128,128]{3,2,1,0:T(8,128)(2,1)}, u32[]{:S(2)}) copy-start(bf16[2,5,128,128]{3,2,1,0:T(8,128)(2,1)} %get-tuple-element.114) | copy-start | bytes 983044
  191.0 19.7 %collective-permute-start.9 = (bf16[2,5,128,128]{3,2,1,0:T(8,128)(2,1)S(1)}, bf16[2,5,128,128]{3,2,1,0:T(8,128)(2,1)S(1)}, u32[]{:S(2)}, u32[]{:S(2)}) collective-permute-start(bf16[2,5,128,128]{3,2,1,0:T(8,128)(2,1)S(1)} %copy-done.24), channel_id=1, source_target_pairs={{0,3},{1,2},{2,1},{3,0},{4,7},{5,6},{6,5},{7,4},{8,11},{9,10},{10,... | collective-permute-start | bytes 983048 | tf_op jit(solution)/shard_map/ppermute | solution.py:673
  196.6 28.7 %copy-start.18 = (bf16[2,5,128,128]{3,2,1,0:T(8,128)(2,1)S(1)}, bf16[2,5,128,128]{3,2,1,0:T(8,128)(2,1)}, u32[]{:S(2)}) copy-start(bf16[2,5,128,128]{3,2,1,0:T(8,128)(2,1)} %get-tuple-element.122) | copy-start | bytes 983044
  196.6 16.4 %collective-permute-start.10 = (bf16[2,5,128,128]{3,2,1,0:T(8,128)(2,1)S(1)}, bf16[2,5,128,128]{3,2,1,0:T(8,128)(2,1)S(1)}, u32[]{:S(2)}, u32[]{:S(2)}) collective-permute-start(bf16[2,5,128,128]{3,2,1,0:T(8,128)(2,1)S(1)} %copy-done.23), channel_id=1, source_target_pairs={{0,1},{1,0},{2,3},{3,2},{4,5},{5,4},{6,7},{7,6},{8,9},{9,8},{10,11... | collective-permute-start | bytes 983048 | tf_op jit(solution)/shard_map/ppermute | solution.py:673
  198.2 20.5 %collective-permute-start.11 = (bf16[2,5,128,128]{3,2,1,0:T(8,128)(2,1)S(1)}, bf16[2,5,128,128]{3,2,1,0:T(8,128)(2,1)S(1)}, u32[]{:S(2)}, u32[]{:S(2)}) collective-permute-start(bf16[2,5,128,128]{3,2,1,0:T(8,128)(2,1)S(1)} %copy-done.22), channel_id=1, source_target_pairs={{0,2},{1,3},{2,0},{3,1},{4,6},{5,7},{6,4},{7,5},{8,10},{9,11},{10,... | collective-permute-start | bytes 983048 | tf_op jit(solution)/shard_map/ppermute | solution.py:673
  204.7 16.5 %collective-permute-start.16 = (bf16[2,5,128,128]{3,2,1,0:T(8,128)(2,1)S(1)}, bf16[2,5,128,128]{3,2,1,0:T(8,128)(2,1)S(1)}, u32[]{:S(2)}, u32[]{:S(2)}) collective-permute-start(bf16[2,5,128,128]{3,2,1,0:T(8,128)(2,1)S(1)} %copy-done.21), channel_id=1, source_target_pairs={{0,1},{1,0},{2,3},{3,2},{4,5},{5,4},{6,7},{7,6},{8,9},{9,8},{10,11... | collective-permute-start | bytes 983048 | tf_op jit(solution)/shard_map/ppermute | solution.py:673
  210.7 14.7 %collective-permute-start.17 = (bf16[2,5,128,128]{3,2,1,0:T(8,128)(2,1)S(1)}, bf16[2,5,128,128]{3,2,1,0:T(8,128)(2,1)S(1)}, u32[]{:S(2)}, u32[]{:S(2)}) collective-permute-start(bf16[2,5,128,128]{3,2,1,0:T(8,128)(2,1)S(1)} %copy-done.20), channel_id=1, source_target_pairs={{0,2},{1,3},{2,0},{3,1},{4,6},{5,7},{6,4},{7,5},{8,10},{9,11},{10,... | collective-permute-start | bytes 983048 | tf_op jit(solution)/shard_map/ppermute | solution.py:673
  212.1 38.7 %copy-start = (bf16[4,2,8,128,128]{4,3,2,1,0:T(8,128)(2,1)S(1)}, bf16[4,2,8,128,128]{4,3,2,1,0:T(8,128)(2,1)}, u32[]{:S(2)}) copy-start(bf16[4,2,8,128,128]{4,3,2,1,0:T(8,128)(2,1)} %get-tuple-element.99.own) | copy-start | bytes 6291460
  212.1 38.7 %copy-start.1 = (bf16[4,2,8,128,128]{4,3,2,1,0:T(8,128)(2,1)S(1)}, bf16[4,2,8,128,128]{4,3,2,1,0:T(8,128)(2,1)}, u32[]{:S(2)}) copy-start(bf16[4,2,8,128,128]{4,3,2,1,0:T(8,128)(2,1)} %get-tuple-element.100.other) | copy-start | bytes 6291460
  213.1 37.7 %collective-permute-start.5 = (bf16[2,8,128,128]{3,2,1,0:T(8,128)(2,1)S(1)}, bf16[2,8,128,128]{3,2,1,0:T(8,128)(2,1)S(1)}, u32[]{:S(2)}, u32[]{:S(2)}) collective-permute-start(bf16[2,8,128,128]{3,2,1,0:T(8,128)(2,1)S(1)} %copy-done.9), channel_id=1, source_target_pairs={{0,8},{4,12},{8,0},{12,4},{1,9},{5,13},{9,1},{13,5},{2,10},{6,14},... | collective-permute-start | bytes 1572872 | tf_op jit(solution)/shard_map/ppermute | solution.py:673
  218.7 32.1 %collective-permute-start.6 = (bf16[2,8,128,128]{3,2,1,0:T(8,128)(2,1)S(1)}, bf16[2,8,128,128]{3,2,1,0:T(8,128)(2,1)S(1)}, u32[]{:S(2)}, u32[]{:S(2)}) collective-permute-start(bf16[2,8,128,128]{3,2,1,0:T(8,128)(2,1)S(1)} %copy-done.7), channel_id=1, source_target_pairs={{0,12},{4,8},{8,4},{12,0},{1,13},{5,9},{9,5},{13,1},{2,14},{6,10},... | collective-permute-start | bytes 1572872 | tf_op jit(solution)/shard_map/ppermute | solution.py:673
  221.2 10.3 %collective-permute-start.12 = (bf16[2,5,128,128]{3,2,1,0:T(8,128)(2,1)S(1)}, bf16[2,5,128,128]{3,2,1,0:T(8,128)(2,1)S(1)}, u32[]{:S(2)}, u32[]{:S(2)}) collective-permute-start(bf16[2,5,128,128]{3,2,1,0:T(8,128)(2,1)S(1)} %copy-done.19), channel_id=1, source_target_pairs={{0,3},{1,2},{2,1},{3,0},{4,7},{5,6},{6,5},{7,4},{8,11},{9,10},{10,... | collective-permute-start | bytes 983048 | tf_op jit(solution)/shard_map/ppermute | solution.py:673
  225.4 12.8 %collective-permute-start.18 = (bf16[2,5,128,128]{3,2,1,0:T(8,128)(2,1)S(1)}, bf16[2,5,128,128]{3,2,1,0:T(8,128)(2,1)S(1)}, u32[]{:S(2)}, u32[]{:S(2)}) collective-permute-start(bf16[2,5,128,128]{3,2,1,0:T(8,128)(2,1)S(1)} %copy-done.18), channel_id=1, source_target_pairs={{0,3},{1,2},{2,1},{3,0},{4,7},{5,6},{6,5},{7,4},{8,11},{9,10},{10,... | collective-permute-start | bytes 983048 | tf_op jit(solution)/shard_map/ppermute | solution.py:673
  (19 other events, 142.8 us)

commit v2 on v1

--- a/solution.py
+++ b/solution.py
@@ -142,7 +142,9 @@
     return (layer_out, grad_tokens, grad_gate, grad_up, grad_down)
 
 
-def gather_kernel(shards, small, both, wg, wu, wd, tok_all, rg, ru, rd, table, *sems):
+def gather_kernel(shards, tokens, cotangent, *refs):
+    rows, factors, (wg, wu, wd), refs = refs[:3], refs[3:6], refs[6:9], refs[9:]
+    tok_all, rg, ru, rd, row_table, factor_table, spot, both, *sems = refs
     (z_send, z_recv, c_send, c_recv, x_send, x_recv, w_send, w_recv, y_send, y_recv, n_send, n_recv, s_send, s_recv, here) = sems
     part, t, f = lax.axis_index("parts"), lax.axis_index("tensor"), lax.axis_index("fsdp")
     flip = [f, (f // 2) * 2 + 1 - f % 2, (f + 2) % 4, ((f + 2) % 4 // 2) * 2 + 1 - f % 2]
@@ -162,6 +164,14 @@
     over = (1 - part, t, f)
     ups = ((part, t + 1, f), (part, t - 1, f))
     more = (t < last, t > 0)
+    spot[0], spot[1] = f, t
+    blk = both.shape[3]
+    for which, ref in enumerate((tokens, cotangent)):
+        for d in range(both.shape[1]):
+            both[which, d] = ref[:, d * blk : (d + 1) * blk]
+    for array in range(3):
+        row_table[0, array] = rows[array][...]
+        factor_table[0, array] = factors[array][...].astype(jnp.float32)
 
     barrier = pltpu.get_barrier_semaphore()
     for m in (1, 2, 3):
@@ -197,7 +207,8 @@
         def _():
             z_copy(way, t, 0, True).start()
     tables = [
-        to(across(m), small.at[flip[m]], table.at[m - 1], s_send.at[m - 1], s_recv.at[m - 1])
+        to(across(m), table.at[0], table.at[m], s_send.at[i, m - 1], s_recv.at[i, m - 1])
+        for i, table in enumerate((row_table, factor_table))
         for m in (1, 2, 3)
     ]
     for c in tables:
@@ -278,28 +289,36 @@
     keep.wait()
 
 
-def gather(small, both, weights, shards):
+def gather(tokens, cotangent, rows, factors, weights, shards):
     per_dev, local_cols, blk, _ = weights[0].shape
     count = local_cols // 4
+    tok, width = tokens.shape
     bf = jnp.bfloat16
     dma = lambda *a: pltpu.SemaphoreType.DMA(a)
     received = jax.ShapeDtypeStruct((3, per_dev, count, blk, blk), bf)
-    anywhere = pl.BlockSpec(memory_space=pl.ANY)
+    anywhere, local = pl.BlockSpec(memory_space=pl.ANY), pl.BlockSpec(memory_space=pltpu.VMEM)
+    both = (2, width // blk, tok, blk)
+    table = (4, 3, per_dev, local_cols)
     z = (2, shards, 2)
     c = (shards, 2)
     one = pltpu.SemaphoreType.DMA
     return pl.pallas_call(
         functools.partial(gather_kernel, shards),
         out_shape=[
-            jax.ShapeDtypeStruct((2, shards, 2) + both.shape, bf),
+            jax.ShapeDtypeStruct((2, shards, 2) + both, bf),
             received, received, received,
-            jax.ShapeDtypeStruct((3,) + small.shape[1:], jnp.float32),
+            jax.ShapeDtypeStruct(table, jnp.int32),
+            jax.ShapeDtypeStruct(table, jnp.float32),
+            jax.ShapeDtypeStruct((2,), jnp.int32),
         ],
-        in_specs=[anywhere] * 5,
-        out_specs=[anywhere] * 5,
-        scratch_shapes=[dma(*z), dma(*z), dma(*c), dma(*c), one, one, dma(6), dma(6), dma(6), dma(6), dma(6), dma(6), dma(3), dma(3), one],
+        in_specs=[local] * 8 + [anywhere] * 3,
+        out_specs=[anywhere] * 4 + [local] * 2 + [pl.BlockSpec(memory_space=pltpu.SMEM)],
+        scratch_shapes=[
+            pltpu.VMEM(both, bf),
+            dma(*z), dma(*z), dma(*c), dma(*c), one, one, dma(6), dma(6), dma(6), dma(6), dma(6), dma(6), dma(2, 3), dma(2, 3), one,
+        ],
         compiler_params=pltpu.CompilerParams(collective_id=0, has_side_effects=True),
-    )(small, both, *weights)
+    )(tokens, cotangent, *rows, *factors, *weights)
 
 
 NN = (((1,), (0,)), ((), ()))
@@ -307,9 +326,14 @@
 dot = functools.partial(lax.dot_general, preferred_element_type=jnp.float32)
 
 
+def entry(table_ref, array, slot, r):
+    per_dev = table_ref.shape[2]
+    return table_ref[slot // per_dev, array, slot % per_dev, r]
+
+
 def load(rows_ref, tok_ref, tok, which, array, slot, r, sel):
     per_shard, blk = tok_ref.shape[4], tok_ref.shape[6]
-    place = rows_ref[array, slot, r]
+    place = entry(rows_ref, array, slot, r)
     shard, block = place // per_shard, place % per_shard
     for c in range(2):
         for x in range(2):
@@ -321,12 +345,12 @@
     per_dev = own.shape[0]
     src, sub = slot // per_dev, slot % per_dev
     value = recv[src - 1, sub, 0] if src else own[sub, 0]
-    return (value.astype(jnp.float32) * scale_ref[array, slot, r]).astype(jnp.bfloat16)
-
-
-def accumulate(rows_ref, acc, array, slots, blk, product):
+    return (value.astype(jnp.float32) * entry(scale_ref, array, slot, r)).astype(jnp.bfloat16)
+
+
+def accumulate(rows_ref, acc, array, slots, r, blk, product):
     for slot in range(slots):
-        acc[rows_ref[array, slot, pl.program_id(0)]] += product[:, slot * blk : (slot + 1) * blk]
+        acc[entry(rows_ref, array, slot, r)] += product[:, slot * blk : (slot + 1) * blk]
 
 
 def clear(acc):
@@ -358,7 +382,7 @@
     grads, (gate_pre_ref, up_pre_ref), refs = refs[:nsrc], refs[nsrc : nsrc + 2], refs[nsrc + 2 :]
     own, other, scratch = refs[:shards], refs[shards : 2 * shards], refs[2 * shards :]
     acc, gate_sel, up_sel, down_sel, gate_w, up_w, down_w = scratch
-    r = pl.program_id(0)
+    r = place_ref[0] * pl.num_programs(0) + pl.program_id(0)
     clear(acc)
     for slot in range(slots):
         span = slice(slot * blk, (slot + 1) * blk)
@@ -375,18 +399,18 @@
     down = dot(hidden.T, down_sel[...], NN)
     for slot in range(slots):
         src, sub = slot // per_dev, slot % per_dev
-        g = down[:, slot * blk : (slot + 1) * blk] * scale_ref[2, slot, r]
+        g = down[:, slot * blk : (slot + 1) * blk] * entry(scale_ref, 2, slot, r)
         grads[src][sub, 0] = g.astype(jnp.bfloat16)
-    accumulate(rows_ref, acc, 2, slots, blk, dot(hidden, down_w[...], NN))
+    accumulate(rows_ref, acc, 2, slots, r, blk, dot(hidden, down_w[...], NN))
     flush(place_ref[1], acc, tok, own, other)
 
 
-def middle_kernel(dims, begin, rows_ref, scale_ref, place_ref, tok_ref, own_w, recv_w, gate_pre_ref, up_pre_ref, *refs):
+def middle_kernel(dims, rows_ref, scale_ref, place_ref, tok_ref, own_w, recv_w, gate_pre_ref, up_pre_ref, *refs):
     slots, per_dev, tok, blk, _ = dims
     nsrc = slots // per_dev
     grads, (gate_act_ref, up_act_ref), scratch = (refs[:nsrc], refs[nsrc : 2 * nsrc]), refs[2 * nsrc : 2 * nsrc + 2], refs[2 * nsrc + 2 :]
     gate_sel, up_sel, down_sel, down_w = scratch
-    r = pl.program_id(0) + begin
+    r = place_ref[0] * pl.num_programs(0) + pl.program_id(0)
     for slot in range(slots):
         load(rows_ref, tok_ref, tok, 0, 0, slot, r, gate_sel)
         load(rows_ref, tok_ref, tok, 0, 1, slot, r, up_sel)
@@ -402,36 +426,32 @@
     for slot in range(slots):
         span = slice(slot * blk, (slot + 1) * blk)
         src, sub = slot // per_dev, slot % per_dev
-        g = dot(gate_sel[:, span].T, gate_act, NN) * scale_ref[0, slot, r]
+        g = dot(gate_sel[:, span].T, gate_act, NN) * entry(scale_ref, 0, slot, r)
         grads[0][src][sub, 0] = g.astype(jnp.bfloat16)
-        g = dot(up_sel[:, span].T, up_act, NN) * scale_ref[1, slot, r]
+        g = dot(up_sel[:, span].T, up_act, NN) * entry(scale_ref, 1, slot, r)
         grads[1][src][sub, 0] = g.astype(jnp.bfloat16)
 
 
-def late_kernel(dims, splits, rows_ref, scale_ref, place_ref, *refs):
-    slots, _, tok, blk, shards = dims
-    own_w, recv_w, refs = refs[:2], refs[2:4], refs[4:]
-    kept, refs = refs[: 2 * len(splits)], refs[2 * len(splits) :]
-    own_ref, other_ref, acc, gate_w, up_w = refs
+def late_kernel(dims, rows_ref, scale_ref, place_ref, *refs):
+    slots, per_dev, tok, blk, shards = dims
+    nsrc = slots // per_dev
+    own_w, recv_w, (gate_act_ref, up_act_ref), pieces, refs = refs[:2], refs[2:4], refs[4:6], refs[6 : 6 + nsrc], refs[6 + nsrc :]
+    own_ref, other_ref, placed_ref, acc, gate_w, up_w = refs
     own, other = [own_ref.at[d] for d in range(shards)], [other_ref.at[d] for d in range(shards)]
-    r = pl.program_id(0)
+    r = place_ref[0] * pl.num_programs(0) + pl.program_id(0)
     clear(acc)
+    for m, piece in enumerate(pieces):
+        placed_ref[:, place_ref[0] ^ m, 0] = piece[:, 0]
     for slot in range(slots):
         span = slice(slot * blk, (slot + 1) * blk)
         gate_w[span, :] = scaled(scale_ref, own_w[0], recv_w[0], 0, slot, r)
         up_w[span, :] = scaled(scale_ref, own_w[1], recv_w[1], 1, slot, r)
-    for i, begin in enumerate(splits):
-        end = splits[i + 1] if i + 1 < len(splits) else pl.num_programs(0)
-
-        @pl.when(jnp.logical_and(r >= begin, r < end))
-        def _():
-            accumulate(rows_ref, acc, 0, slots, blk, dot(kept[2 * i][0], gate_w[...], NT))
-            accumulate(rows_ref, acc, 1, slots, blk, dot(kept[2 * i + 1][0], up_w[...], NT))
-
+    accumulate(rows_ref, acc, 0, slots, r, blk, dot(gate_act_ref[0], gate_w[...], NT))
+    accumulate(rows_ref, acc, 1, slots, r, blk, dot(up_act_ref[0], up_w[...], NT))
     flush(0, acc, tok, own, other)
 
 
-def columns(which, scalars, tok_all, own_w, recv_w, kept, splits):
+def columns(which, scalars, tok_all, own_w, recv_w, kept):
     nsrc = 1 + recv_w[0].shape[0]
     _, per_dev, count, blk, _ = recv_w[0].shape
     _, shards, _, _, per_shard, tok, _ = tok_all.shape
@@ -439,15 +459,13 @@
     slots = per_dev * nsrc
     total = 4 * tok
     bf, f32 = jnp.bfloat16, jnp.float32
-    ends = splits[1:] + (count,)
-    begin, steps = (splits[which], ends[which] - splits[which]) if isinstance(which, int) else (0, count)
     whole = lambda a: pl.BlockSpec(a, lambda r, *_: (0,) * len(a), pipeline_mode=pl.Buffered(1))
-    own_block = pl.BlockSpec((per_dev, 1, blk, blk), lambda r, rows, scale, at: (0, at[0] * count + begin + r, 0, 0))
-    recv_block = pl.BlockSpec((nsrc - 1, per_dev, 1, blk, blk), lambda r, *_: (0, 0, begin + r, 0, 0))
+    own_block = pl.BlockSpec((per_dev, 1, blk, blk), lambda r, rows, scale, at: (0, at[0] * count + r, 0, 0))
+    recv_block = pl.BlockSpec((nsrc - 1, per_dev, 1, blk, blk), lambda r, *_: (0, 0, r, 0, 0))
     block = pl.BlockSpec((per_dev, 1, blk, blk), lambda r, *_: (0, r, 0, 0))
-    piece = jax.ShapeDtypeStruct((per_dev, steps, blk, blk), bf)
-    clipped = lambda low, size: pl.BlockSpec((1, total, blk), lambda r, *_: (jnp.clip(r - low, 0, size - 1), 0, 0))
-    keep = lambda kind: [jax.ShapeDtypeStruct((steps, total, blk), kind)] * 2
+    piece = jax.ShapeDtypeStruct((per_dev, count, blk, blk), bf)
+    kept_block = [pl.BlockSpec((1, total, blk), lambda r, *_: (r, 0, 0))] * 2
+    keep = lambda kind: [jax.ShapeDtypeStruct((count, total, blk), kind)] * 2
     share = (2, per_shard, tok, blk)
     acc = pltpu.VMEM((nblk, total, blk), f32)
     sel = pltpu.VMEM((total, slots * blk), bf)
@@ -457,51 +475,61 @@
         body, products = functools.partial(early_kernel, dims), 4
         in_specs = [whole(tok_all.shape)] + [own_block] * 3 + [recv_block] * 3
         operands = (tok_all, *own_w, *recv_w)
-        out_specs = [block] * nsrc + [clipped(0, count)] * 2 + [whole(share)] * (2 * shards)
+        out_specs = [block] * nsrc + kept_block + [whole(share)] * (2 * shards)
         out_shape = [piece] * nsrc + keep(f32) + [jax.ShapeDtypeStruct(share, bf)] * (2 * shards)
         scratch = [acc, sel, sel, sel, tall, tall, wide]
     elif which == "late":
-        body, products = functools.partial(late_kernel, dims, splits), 2
-        in_specs = [own_block] * 2 + [recv_block] * 2
-        for low, high in zip(splits, ends):
-            in_specs += [clipped(low, high - low)] * 2
+        body, products = functools.partial(late_kernel, dims), 2
+        in_specs = [own_block] * 2 + [recv_block] * 2 + kept_block + [block] * nsrc
         operands = (*own_w[:2], *recv_w[:2], *kept)
-        out_specs, out_shape = [whole((shards,) + share)] * 2, [jax.ShapeDtypeStruct((shards,) + share, bf)] * 2
+        placed = pl.BlockSpec((per_dev, nsrc, 1, blk, blk), lambda r, *_: (0, 0, r, 0, 0))
+        out_specs = [whole((shards,) + share)] * 2 + [placed]
+        out_shape = [jax.ShapeDtypeStruct((shards,) + share, bf)] * 2
+        out_shape += [jax.ShapeDtypeStruct((per_dev, nsrc, count, blk, blk), bf)]
         scratch = [acc, tall, tall]
     else:
-        body, products = functools.partial(middle_kernel, dims, begin), 3
-        pre = pl.BlockSpec((1, total, blk), lambda r, *_: (begin + r, 0, 0))
-        in_specs = [whole(tok_all.shape), own_block, recv_block] + [pre] * 2
+        body, products = functools.partial(middle_kernel, dims), 3
+        in_specs = [whole(tok_all.shape), own_block, recv_block] + kept_block
         operands = (tok_all, own_w[2], recv_w[2], *kept)
-        out_specs, out_shape = [block] * (2 * nsrc) + [clipped(0, steps)] * 2, [piece] * (2 * nsrc) + keep(bf)
+        out_specs, out_shape = [block] * (2 * nsrc) + kept_block, [piece] * (2 * nsrc) + keep(bf)
         scratch = [sel, sel, sel, wide]
-    flops = 2 * products * slots * steps * total * blk * blk
+    flops = 2 * products * slots * count * total * blk * blk
     return pl.pallas_call(
         body,
         grid_spec=pltpu.PrefetchScalarGridSpec(
-            num_scalar_prefetch=3, grid=(steps,), in_specs=in_specs, out_specs=out_specs, scratch_shapes=scratch,
+            num_scalar_prefetch=3, grid=(count,), in_specs=in_specs, out_specs=out_specs, scratch_shapes=scratch,
         ),
         out_shape=out_shape,
-        compiler_params=pltpu.CompilerParams(vmem_limit_bytes=60 * 1024 * 1024),
+        compiler_params=pltpu.CompilerParams(vmem_limit_bytes=64_600_000 if which == "late" else 60 * 1024 * 1024),
         cost_estimate=pl.CostEstimate(flops=flops, bytes_accessed=40 << 20, transcendentals=0),
     )(*scalars, *operands)
 
 
 def add_kernel(pairs, *refs):
-    for a, b, out in zip(refs[:pairs], refs[pairs : 2 * pairs], refs[2 * pairs :]):
-        out[...] = (a[...].astype(jnp.float32) + b[...].astype(jnp.float32)).astype(out.dtype)
+    left, right, out, (held, load_sem, store_sem) = refs[:pairs], refs[pairs : 2 * pairs], refs[2 * pairs : 3 * pairs], refs[3 * pairs :]
+    loads = [pltpu.make_async_copy(a, held.at[0, m], load_sem.at[m]) for m, a in enumerate(left)]
+    stores = [pltpu.make_async_copy(held.at[1, m], c, store_sem.at[m]) for m, c in enumerate(out)]
+    for c in loads:
+        c.start()
+    for m in reversed(range(pairs)):
+        loads[m].wait()
+        held[1, m] = (held[0, m].astype(jnp.float32) + right[m][...].astype(jnp.float32)).astype(held.dtype)
+        stores[m].start()
+    for c in stores:
+        c.wait()
 
 
 def add_pairs(left, right):
-    pairs, (near, blocks, tok, blk) = len(left), left[0].shape
-    spec = pl.BlockSpec((1, blocks // 2, tok, blk), lambda i, j: (i, j, 0, 0))
+    pairs, unit = len(left), left[0]
+    stay, local = pl.BlockSpec(memory_space=pltpu.HBM), pl.BlockSpec(memory_space=pltpu.VMEM)
+    dma = pltpu.SemaphoreType.DMA((pairs,))
     return pl.pallas_call(
         functools.partial(add_kernel, pairs),
-        grid=(near, 2),
-        in_specs=[spec] * (2 * pairs),
-        out_specs=[spec] * pairs,
-        out_shape=[jax.ShapeDtypeStruct(left[0].shape, left[0].dtype)] * pairs,
-        compiler_params=pltpu.CompilerParams(vmem_limit_bytes=32 * 1024 * 1024),
+        in_specs=[stay] * pairs + [local] * pairs,
+        out_specs=[stay] * pairs,
+        out_shape=[jax.ShapeDtypeStruct(unit.shape, unit.dtype)] * pairs,
+        scratch_shapes=[pltpu.VMEM((2, pairs) + unit.shape, unit.dtype), dma, dma],
+        compiler_params=pltpu.CompilerParams(vmem_limit_bytes=64_600_000),
     )(*left, *right)
 
 
@@ -665,8 +693,50 @@
             pltpu.VMEM(pair + unit, bf),
             dma(*pair), dma(*pair), dma(*pair), dma(2, *pair), dma(2, *pair), dma(2), dma(2), dma(shards),
         ],
-        compiler_params=pltpu.CompilerParams(collective_id=1, has_side_effects=True, vmem_limit_bytes=24 * 1024 * 1024),
+        compiler_params=pltpu.CompilerParams(collective_id=1, has_side_effects=True, vmem_limit_bytes=66_400_000),
     )(own, other, *shares)
+
+
+def home_kernel(arrays, place_ref, *refs):
+    nsrc = (len(refs) - 3) // arrays - 1
+    pieces, placed, (held, load_sem, store_sem) = refs[: arrays * nsrc], refs[arrays * nsrc : -3], refs[-3:]
+    count = held.shape[2]
+    loads, stores = [], []
+    for j, piece in enumerate(pieces):
+        array, m = j // nsrc, j % nsrc
+        for sub in range(piece.shape[0]):
+            column = (place_ref[0] ^ m) * count
+            loads.append(pltpu.make_async_copy(piece.at[sub], held.at[j, sub], load_sem.at[j, sub]))
+            stores.append(
+                pltpu.make_async_copy(held.at[j, sub], placed[array].at[sub, pl.ds(column, count)], store_sem.at[j, sub])
+            )
+    for c in loads:
+        c.start()
+    for a, b in zip(loads, stores):
+        a.wait()
+        b.start()
+    for c in stores:
+        c.wait()
+
+
+def home(place, sent):
+    arrays, nsrc = len(sent), len(sent[0])
+    per_dev, count, blk, _ = sent[0][0].shape
+    anywhere = pl.BlockSpec(memory_space=pl.ANY)
+    shape = jax.ShapeDtypeStruct((per_dev, nsrc * count, blk, blk), sent[0][0].dtype)
+    held = (arrays * nsrc, per_dev)
+    return pl.pallas_call(
+        functools.partial(home_kernel, arrays),
+        grid_spec=pltpu.PrefetchScalarGridSpec(
+            num_scalar_prefetch=1, grid=(1,),
+            in_specs=[anywhere] * (arrays * nsrc), out_specs=[anywhere] * arrays,
+            scratch_shapes=[
+                pltpu.VMEM(held + (count, blk, blk), sent[0][0].dtype), pltpu.SemaphoreType.DMA(held), pltpu.SemaphoreType.DMA(held),
+            ],
+        ),
+        out_shape=[shape] * arrays,
+        compiler_params=pltpu.CompilerParams(vmem_limit_bytes=66_400_000),
+    )(place, *[piece for pieces in sent for piece in pieces])
 
 
 def swap(value, flip, axis="fsdp"):
@@ -686,53 +756,28 @@
     down_cols,
     down_scale,
 ):
-    tok, width = tokens.shape
-    per_dev, local_cols, blk, _ = gate_values.shape
-    count = local_cols // 4
-    mine, shard = lax.axis_index("fsdp"), lax.axis_index("tensor")
-    f32, bf = jnp.float32, jnp.bfloat16
-
+    _, width = tokens.shape
     shards = lax.axis_size("tensor")
-    both = jnp.stack([tokens, cotangent]).reshape(2, tok, width // blk, blk).transpose(0, 2, 1, 3)
-    small = jnp.stack(
-        [a.astype(f32) for a in (gate_rows, up_rows, down_cols, gate_scale, up_scale, down_scale)]
-    )
-    small = small.reshape(6, per_dev, 4, count).transpose(2, 0, 1, 3)
     own_w = (gate_values, up_values, down_values)
-    tok_all, *recv_w, table = gather(small, both, own_w, shards)
-    kept = lax.dynamic_slice_in_dim(small, mine, 1, axis=0)
-    table = jnp.concatenate([kept, table]).transpose(1, 0, 2, 3).reshape(6, 4 * per_dev, count)
-    table_rows = table[:3].astype(jnp.int32)
-    table_scale = table[3:]
-    splits = (0, (count + 1) // 2)
-
-    def home(parts):
-        result = jnp.zeros((per_dev, local_cols, blk, blk), bf)
-        for begin, pieces in parts:
-            for m, piece in enumerate(pieces):
-                result = lax.dynamic_update_slice_in_dim(result, piece, (mine ^ m) * count + begin, axis=1)
-        return result
+    rows, factors = (gate_rows, up_rows, down_cols), (gate_scale, up_scale, down_scale)
+    tok_all, *recv_w, row_table, factor_table, place = gather(tokens, cotangent, rows, factors, own_w, shards)
+    scalars = (row_table, factor_table, place)
 
     def send(pieces):
         return [p if m == 0 else swap(p, m) for m, p in enumerate(pieces)]
 
-    scalars = (table_rows, table_scale, jnp.stack([mine, shard]).astype(jnp.int32))
-    early = columns("early", scalars, tok_all, own_w, recv_w, (), splits)
+    early = columns("early", scalars, tok_all, own_w, recv_w, ())
     down_pieces, pre, own, other = early[:4], early[4:6], early[6 : 6 + shards], early[6 + shards :]
     chip = add_pairs(own, [swap(b, 1) for b in other])
     down_sent = send(down_pieces)
     chip, pre = lax.optimization_barrier((chip, pre))
     out_shares = [c if m == 0 else swap(c, m, "tensor") for m, c in enumerate(chip)]
-    acts, gate_sent, up_sent = [], [], []
-    for i, begin in enumerate(splits):
-        middle = columns(i, scalars, tok_all, own_w, recv_w, pre, splits)
-        gate_sent.append((begin, send(middle[:4])))
-        up_sent.append((begin, send(middle[4:8])))
-        acts += middle[8:]
-        pre, acts = lax.optimization_barrier((pre, acts))
-    own, other = columns("late", scalars, tok_all, own_w, recv_w, acts, splits)
+    middle = columns("middle", scalars, tok_all, own_w, recv_w, pre)
+    gate_sent, up_sent = send(middle[:4]), send(middle[4:8])
+    own, other, grad_down = columns("late", scalars, tok_all, own_w, recv_w, (*middle[8:], *down_sent))
     layer_out, grad_tokens = reduce(own, other, out_shares, width)
-    return (layer_out, grad_tokens, home(gate_sent), home(up_sent), home([(0, down_sent)]))
+    grad_gate, grad_up = home(place, (gate_sent, up_sent))
+    return (layer_out, grad_tokens, grad_gate, grad_up, grad_down.reshape(gate_values.shape))
 
 
 def choose_plan(mesh, *args):

time: 303 us -> 256 us (0.84)
  local copies, waits for them, and re-layouts: 34.6 us -> 2.24 us
  waiting for transfers between devices: 41.8 us -> 33.5 us
  starting transfers between devices: 15.9 us -> 11.4 us
  other arithmetic: 4.3 us -> 0 us
    dynamic_update_slice x19 -> x0, local copies, waits for them, and re-layouts: 19.5 us -> none  [home(): lax.dynamic_update_slice_in_dim(result, piece, (mine ^ m) * count + begin...]
    ppermute x22 -> x16, waiting for transfers between devices: 41.8 us -> 33.5 us  [swap(): lax.ppermute(value, axis, [(i, i ^ flip) for i in range(lax.axis_size(axi...]
    pallas_call x1 -> x2, Pallas kernels: 2.42 us -> 10.3 us  [the longest x1 5.73 us: home(): pl.pallas_call(functools.partial(home_kernel, arrays), grid_spec=pltpu.Pr...]
    another operation x12 -> x0, local copies, waits for them, and re-layouts: 7.74 us -> none
    pallas_call x4 -> x3, Pallas kernels: 74.8 us -> 69.3 us  [columns(): pl.pallas_call(body, grid_spec=pltpu.PrefetchScalarGridSpec(num_scalar_pr...]
    ppermute x22 -> x16, starting transfers between devices: 15.9 us -> 11.4 us  [swap(): lax.ppermute(value, axis, [(i, i ^ flip) for i in range(lax.axis_size(axi...]
    unnamed x67 -> x22, local copies, waits for them, and re-layouts: 6.21 us -> 2.24 us
  transfers between devices with their start and end apart: 22 -> 16, of which waited for: 8 -> 3; matrix products, arithmetic and copies ran while one was open for 8% -> 0% of each run, Pallas kernels for 17% -> 38%
where the time goes in v2:
time: 256 us; the launch traced here: 254 us
  Pallas kernels  206 us (80%)
  waiting for transfers between devices  33.5 us (13%)
  starting transfers between devices  11.4 us (4%)
    pallas_call x1, Pallas kernels, gather(): pl.pallas_call(functools.partial(gather_kernel, shards), out_shape=[jax.S...  78.9 us
    pallas_call x3, Pallas kernels, columns(): pl.pallas_call(body, grid_spec=pltpu.PrefetchScalarGridSpec(num_scalar_pr...  69.3 us
    pallas_call x1, Pallas kernels, reduce(): pl.pallas_call(functools.partial(reduce_kernel, shards), out_shape=[jax.S...  47.8 us
    ppermute x16, waiting for transfers between devices, swap(): lax.ppermute(value, axis, [(i, i ^ flip) for i in range(lax.axis_size(axi...  33.5 us
    ppermute x16, starting transfers between devices, swap(): lax.ppermute(value, axis, [(i, i ^ flip) for i in range(lax.axis_size(axi...  11.4 us
    pallas_call x1, Pallas kernels, home(): pl.pallas_call(functools.partial(home_kernel, arrays), grid_spec=pltpu.Pr...  5.73 us
  transfers between devices with their start and end apart: 16, of which 3 were waited for; matrix products, arithmetic and copies ran while one was open for 0% of the time, Pallas kernels for 38%

profile of v2, /device:TPU:0, one launch (start us, length us, event | category | flops | bytes accessed | tf_op | source)
XLA Modules:
  0.0 254.3 jit_solution(10691295374876832776)
XLA Ops:
  0.6 78.9 %shard_map.146 = (bf16[2,4,2,2,8,128,128]{6,5,4,3,2,1,0:T(8,128)(2,1)}, bf16[3,2,10,128,128]{4,3,2,1,0:T(8,128)(2,1)}, bf16[3,2,10,128,128]{4,3,2,1,0:T(8,128)(2...) custom-call(bf16[128,1024]{1,0:T(8,128)(2,1)} %tokens.1, ...), custom_call_target="tpu_custom_call" | custom-call | tf_op jit(solution)/shard_map/pallas_call | solution.py:305
  79.5 25.6 %shard_map.147 = (bf16[2,10,128,128]{3,2,1,0:T(8,128)(2,1)}, bf16[2,10,128,128]{3,2,1,0:T(8,128)(2,1)}, bf16[2,10,128,128]{3,2,1,0:T(8,128)(2,1)}, bf16[2,10,128...) custom-call(s32[4,3,2,40]{3,2,1,0:T(2,128)} %get-tuple-element.53.ro, ...), custom_call_target="tpu_custom_call" | custom-call | flops 5368709120 | bytes 41943040 | tf_op jit(solution)/shard_map/pallas_call | solution.py:497
  105.1 0.4 collective-permute-start
  105.6 0.1 collective-permute-start.1
  105.7 0.4 collective-permute-start.2
  106.1 0.1 collective-permute-start.3
  106.2 0.4 collective-permute-start.4
  106.6 0.7 collective-permute-done.refs_4_
  107.3 1.4 collective-permute-start.5
  108.8 0.8 copy-done.4
  109.6 0.8 collective-permute-start.6
  110.3 4.6 %shard_map.148 = (bf16[2,8,128,128]{3,2,1,0:T(8,128)(2,1)}, bf16[2,8,128,128]{3,2,1,0:T(8,128)(2,1)}, bf16[2,8,128,128]{3,2,1,0:T(8,128)(2,1)}, bf16[2,8,128,128]{3,2,1,0:T(8,128)(2,1)}) custom-call(bf16[2,8,128,128]{3,2,1,0:T(8,128)(2,1)} %get-tuple-element.60.refs_0_, bf16[2,8,128,128]{3,2,1,0:T(8,128)(2,1)} %get-tuple-element.61.refs_1_, ...), custom_call_target="tpu_custom_call" | custom-call | tf_op jit(solution)/shard_map/pallas_call | solution.py:526
  115.0 26.7 %shard_map.149 = (bf16[2,10,128,128]{3,2,1,0:T(8,128)(2,1)}, bf16[2,10,128,128]{3,2,1,0:T(8,128)(2,1)}, bf16[2,10,128,128]{3,2,1,0:T(8,128)(2,1)}, bf16[2,10,128...) custom-call(s32[4,3,2,40]{3,2,1,0:T(2,128)} %get-tuple-element.53.ro, ...), custom_call_target="tpu_custom_call" | custom-call | flops 4026531840 | bytes 41943040 | tf_op jit(solution)/shard_map/pallas_call | solution.py:497
  141.7 0.2 collective-permute-start.10
  141.9 3.1 %collective-permute-start.8 = (bf16[2,8,128,128]{3,2,1,0:T(8,128)(2,1)S(1)}, bf16[2,8,128,128]{3,2,1,0:T(8,128)(2,1)}, u32[]{:S(2)}, u32[]{:S(2)}) collective-permute-start(bf16[2,8,128,128]{3,2,1,0:T(8,128)(2,1)S(1)} %copy-done.8), channel_id=1, source_target_pairs={{0,8},{4,12},{8,0},{12,4},{1,9},{5,13},{9,1},{13,5},{2,10},{6,14},... | collective-permute-start | bytes 1572872 | tf_op jit(solution)/shard_map/ppermute | solution.py:743
  145.0 0.0 collective-permute-done.5.refs_8_
  145.0 1.4 collective-permute-start.9
  146.4 0.0 collective-permute-done.6.refs_9_
  146.4 1.2 collective-permute-start.11
  147.7 19.3 %collective-permute-done.7.refs_0_ = bf16[2,8,128,128]{3,2,1,0:T(8,128)(2,1)} collective-permute-done((bf16[2,8,128,128]{3,2,1,0:T(8,128)(2,1)S(1)}, bf16[2,8,128,128]{3,2,1,0:T(8,128)(2,1)}, u32[]{:S(2)}, u32[]{:S(2)}) %collective-permute-start.7) | collective-permute-done | bytes 524320 | tf_op jit(solution)/shard_map/ppermute | solution.py:743
  167.0 0.0 collective-permute-start.12
  167.0 13.4 %collective-permute-done.8.refs_1_ = bf16[2,8,128,128]{3,2,1,0:T(8,128)(2,1)} collective-permute-done((bf16[2,8,128,128]{3,2,1,0:T(8,128)(2,1)S(1)}, bf16[2,8,128,128]{3,2,1,0:T(8,128)(2,1)}, u32[]{:S(2)}, u32[]{:S(2)}) %collective-permute-start.8) | collective-permute-done | bytes 524320 | tf_op jit(solution)/shard_map/ppermute | solution.py:743
  180.4 0.0 collective-permute-start.13
  180.4 0.0 collective-permute-done.9.refs_2_
  180.4 1.2 collective-permute-start.14
  181.6 0.0 collective-permute-done.10.refs_1_
  181.6 0.6 collective-permute-start.15
  182.3 17.0 %shard_map.150 = (bf16[4,2,8,128,128]{4,3,2,1,0:T(8,128)(2,1)}, bf16[4,2,8,128,128]{4,3,2,1,0:T(8,128)(2,1)}, bf16[2,4,10,128,128]{4,3,2,1,0:T(8,128)(2,1)}) custom-call(s32[4,3,2,40]{3,2,1,0:T(2,128)} %get-tuple-element.53.rows_ref, f32[4,3,2,40]{3,2,1,0:T(2,128)} %get-tuple-element.54.scale_ref, s32[2]{0:T(128)} %get-tuple-element.55.place_ref, ...), custom_call_target="tpu_custom_call" | custom-call | flops 2684354560 | bytes 41943040 | tf_op jit(solution)/shard_map/pallas_call | solution.py:497
  199.3 47.8 %shard_map.151 = (bf16[128,1024]{1,0:T(8,128)(2,1)}, bf16[128,1024]{1,0:T(8,128)(2,1)}) custom-call(bf16[4,2,8,128,128]{4,3,2,1,0:T(8,128)(2,1)} %get-tuple-element.82.own, bf16[4,2,8,128,128]{4,3,2,1,0:T(8,128)(2,1)} %get-tuple-element.83.other, bf16[2,8,128,128]{3,2,1,0:T(8,128)(2,1)} %get-tuple-element.84.first, ...), custom_call_target="tpu_custom_call" | custom-call | tf_op jit(solution)/shard_map/pallas_call | solution.py:685
  247.1 5.7 %shard_map.152 = (bf16[2,40,128,128]{3,2,1,0:T(8,128)(2,1)}, bf16[2,40,128,128]{3,2,1,0:T(8,128)(2,1)}) custom-call(s32[2]{0:T(128)} %get-tuple-element.55.place_ref, bf16[2,10,128,128]{3,2,1,0:T(8,128)(2,1)} %get-tuple-element.90.refs_0_, bf16[2,10,128,128]{3,2,1,0:T(8,128)(2,1)} %collective-permute-done.10.refs_1_, ...), custom_call_target="tpu_custom_call" | custom-call | tf_op jit(solution)/shard_map/pallas_call | solution.py:728
  252.9 0.7 copy.18
  253.6 0.7 copy.19
  (29 shorter events, 0.1 us)
Async XLA Ops:
  105.1 2.2 collective-permute-start
  105.6 3.2 %collective-permute-start.1 = (bf16[2,8,128,128]{3,2,1,0:T(8,128)(2,1)}, bf16[2,8,128,128]{3,2,1,0:T(8,128)(2,1)S(1)}, u32[]{:S(2)}, u32[]{:S(2)}) collective-permute-start(bf16[2,8,128,128]{3,2,1,0:T(8,128)(2,1)} %get-tuple-element.65), channel_id=1, source_target_pairs={{0,1},{1,0},{2,3},{3,2},{4,5},{5,4},{6,7},{7,6},{8,9},{9,8},{10,11... | collective-permute-start | bytes 1572872 | tf_op jit(solution)/shard_map/ppermute | solution.py:743
  105.7 4.6 %collective-permute-start.2 = (bf16[2,8,128,128]{3,2,1,0:T(8,128)(2,1)}, bf16[2,8,128,128]{3,2,1,0:T(8,128)(2,1)}, u32[]{:S(2)}, u32[]{:S(2)}) collective-permute-start(bf16[2,8,128,128]{3,2,1,0:T(8,128)(2,1)} %get-tuple-element.66), channel_id=1, source_target_pairs={{0,1},{1,0},{2,3},{3,2},{4,5},{5,4},{6,7},{7,6},{8,9},{9,8},{10,11... | collective-permute-start | bytes 1572872 | tf_op jit(solution)/shard_map/ppermute | solution.py:743
  106.1 4.2 %collective-permute-start.3 = (bf16[2,8,128,128]{3,2,1,0:T(8,128)(2,1)}, bf16[2,8,128,128]{3,2,1,0:T(8,128)(2,1)}, u32[]{:S(2)}, u32[]{:S(2)}) collective-permute-start(bf16[2,8,128,128]{3,2,1,0:T(8,128)(2,1)} %get-tuple-element.67), channel_id=1, source_target_pairs={{0,1},{1,0},{2,3},{3,2},{4,5},{5,4},{6,7},{7,6},{8,9},{9,8},{10,11... | collective-permute-start | bytes 1572872 | tf_op jit(solution)/shard_map/ppermute | solution.py:743
  106.2 35.7 %collective-permute-start.4 = (bf16[2,10,128,128]{3,2,1,0:T(8,128)(2,1)}, bf16[2,10,128,128]{3,2,1,0:T(8,128)(2,1)S(1)}, u32[]{:S(2)}, u32[]{:S(2)}) collective-permute-start(bf16[2,10,128,128]{3,2,1,0:T(8,128)(2,1)} %get-tuple-element.79), channel_id=1, source_target_pairs={{0,1},{1,0},{2,3},{3,2},{4,5},{5,4},{6,7},{7,6},{8,9},{9,8},{10,11... | collective-permute-start | bytes 1966088 | tf_op jit(solution)/shard_map/ppermute | solution.py:743
  107.3 1.4 copy-start.3
  107.3 37.7 %collective-permute-start.5 = (bf16[2,10,128,128]{3,2,1,0:T(8,128)(2,1)}, bf16[2,10,128,128]{3,2,1,0:T(8,128)(2,1)S(1)}, u32[]{:S(2)}, u32[]{:S(2)}) collective-permute-start(bf16[2,10,128,128]{3,2,1,0:T(8,128)(2,1)} %get-tuple-element.80), channel_id=1, source_target_pairs={{0,2},{1,3},{2,0},{3,1},{4,6},{5,7},{6,4},{7,5},{8,10},{9,11},{10,... | collective-permute-start | bytes 1966088 | tf_op jit(solution)/shard_map/ppermute | solution.py:743
  108.8 0.8 copy-start.4
  109.6 36.9 %collective-permute-start.6 = (bf16[2,10,128,128]{3,2,1,0:T(8,128)(2,1)}, bf16[2,10,128,128]{3,2,1,0:T(8,128)(2,1)S(1)}, u32[]{:S(2)}, u32[]{:S(2)}) collective-permute-start(bf16[2,10,128,128]{3,2,1,0:T(8,128)(2,1)} %get-tuple-element.81), channel_id=1, source_target_pairs={{0,3},{1,2},{2,1},{3,0},{4,7},{5,6},{6,5},{7,4},{8,11},{9,10},{10,... | collective-permute-start | bytes 1966088 | tf_op jit(solution)/shard_map/ppermute | solution.py:743
  114.9 27.0 %copy-start.9 = (bf16[2,8,128,128]{3,2,1,0:T(8,128)(2,1)S(1)}, bf16[2,8,128,128]{3,2,1,0:T(8,128)(2,1)}, u32[]{:S(2)}) copy-start(bf16[2,8,128,128]{3,2,1,0:T(8,128)(2,1)} %get-tuple-element.85) | copy-start | bytes 1572868
  114.9 27.0 %copy-start.8 = (bf16[2,8,128,128]{3,2,1,0:T(8,128)(2,1)S(1)}, bf16[2,8,128,128]{3,2,1,0:T(8,128)(2,1)}, u32[]{:S(2)}) copy-start(bf16[2,8,128,128]{3,2,1,0:T(8,128)(2,1)} %get-tuple-element.86) | copy-start | bytes 1572868
  114.9 30.1 %copy-start.7 = (bf16[2,8,128,128]{3,2,1,0:T(8,128)(2,1)S(1)}, bf16[2,8,128,128]{3,2,1,0:T(8,128)(2,1)}, u32[]{:S(2)}) copy-start(bf16[2,8,128,128]{3,2,1,0:T(8,128)(2,1)} %get-tuple-element.87) | copy-start | bytes 1572868
  141.7 39.9 %collective-permute-start.10 = (bf16[2,10,128,128]{3,2,1,0:T(8,128)(2,1)}, bf16[2,10,128,128]{3,2,1,0:T(8,128)(2,1)}, u32[]{:S(2)}, u32[]{:S(2)}) collective-permute-start(bf16[2,10,128,128]{3,2,1,0:T(8,128)(2,1)} %get-tuple-element.91), channel_id=1, source_target_pairs={{0,1},{1,0},{2,3},{3,2},{4,5},{5,4},{6,7},{7,6},{8,9},{9,8},{10,11... | collective-permute-start | bytes 1966088 | tf_op jit(solution)/shard_map/ppermute | solution.py:743
  141.9 25.1 %collective-permute-start.7 = (bf16[2,8,128,128]{3,2,1,0:T(8,128)(2,1)S(1)}, bf16[2,8,128,128]{3,2,1,0:T(8,128)(2,1)}, u32[]{:S(2)}, u32[]{:S(2)}) collective-permute-start(bf16[2,8,128,128]{3,2,1,0:T(8,128)(2,1)S(1)} %copy-done.9), channel_id=1, source_target_pairs={{0,4},{4,0},{8,12},{12,8},{1,5},{5,1},{9,13},{13,9},{2,6},{6,2},{1... | collective-permute-start | bytes 1572872 | tf_op jit(solution)/shard_map/ppermute | solution.py:743
  141.9 40.4 %copy-start = (bf16[2,10,128,128]{3,2,1,0:T(8,128)(2,1)}, bf16[2,10,128,128]{3,2,1,0:T(8,128)(2,1)S(1)}, u32[]{:S(2)}) copy-start(bf16[2,10,128,128]{3,2,1,0:T(8,128)(2,1)S(1)} %collective-permute-done.4.refs_7_) | copy-start | bytes 1966084
  141.9 38.5 %collective-permute-start.8 = (bf16[2,8,128,128]{3,2,1,0:T(8,128)(2,1)S(1)}, bf16[2,8,128,128]{3,2,1,0:T(8,128)(2,1)}, u32[]{:S(2)}, u32[]{:S(2)}) collective-permute-start(bf16[2,8,128,128]{3,2,1,0:T(8,128)(2,1)S(1)} %copy-done.8), channel_id=1, source_target_pairs={{0,8},{4,12},{8,0},{12,4},{1,9},{5,13},{9,1},{13,5},{2,10},{6,14},... | collective-permute-start | bytes 1572872 | tf_op jit(solution)/shard_map/ppermute | solution.py:743
  145.0 37.3 %copy-start.1 = (bf16[2,10,128,128]{3,2,1,0:T(8,128)(2,1)}, bf16[2,10,128,128]{3,2,1,0:T(8,128)(2,1)S(1)}, u32[]{:S(2)}) copy-start(bf16[2,10,128,128]{3,2,1,0:T(8,128)(2,1)S(1)} %collective-permute-done.5.refs_8_) | copy-start | bytes 1966084
  145.0 35.4 %collective-permute-start.9 = (bf16[2,8,128,128]{3,2,1,0:T(8,128)(2,1)S(1)}, bf16[2,8,128,128]{3,2,1,0:T(8,128)(2,1)}, u32[]{:S(2)}, u32[]{:S(2)}) collective-permute-start(bf16[2,8,128,128]{3,2,1,0:T(8,128)(2,1)S(1)} %copy-done.7), channel_id=1, source_target_pairs={{0,12},{4,8},{8,4},{12,0},{1,13},{5,9},{9,5},{13,1},{2,14},{6,10},... | collective-permute-start | bytes 1572872 | tf_op jit(solution)/shard_map/ppermute | solution.py:743
  146.4 35.8 %copy-start.2 = (bf16[2,10,128,128]{3,2,1,0:T(8,128)(2,1)}, bf16[2,10,128,128]{3,2,1,0:T(8,128)(2,1)S(1)}, u32[]{:S(2)}) copy-start(bf16[2,10,128,128]{3,2,1,0:T(8,128)(2,1)S(1)} %collective-permute-done.6.refs_9_) | copy-start | bytes 1966084
  146.4 100.6 %collective-permute-start.11 = (bf16[2,10,128,128]{3,2,1,0:T(8,128)(2,1)}, bf16[2,10,128,128]{3,2,1,0:T(8,128)(2,1)}, u32[]{:S(2)}, u32[]{:S(2)}) collective-permute-start(bf16[2,10,128,128]{3,2,1,0:T(8,128)(2,1)} %get-tuple-element.92), channel_id=1, source_target_pairs={{0,2},{1,3},{2,0},{3,1},{4,6},{5,7},{6,4},{7,5},{8,10},{9,11},{10,... | collective-permute-start | bytes 1966088 | tf_op jit(solution)/shard_map/ppermute | solution.py:743
  167.0 80.1 %collective-permute-start.12 = (bf16[2,10,128,128]{3,2,1,0:T(8,128)(2,1)}, bf16[2,10,128,128]{3,2,1,0:T(8,128)(2,1)}, u32[]{:S(2)}, u32[]{:S(2)}) collective-permute-start(bf16[2,10,128,128]{3,2,1,0:T(8,128)(2,1)} %get-tuple-element.93), channel_id=1, source_target_pairs={{0,3},{1,2},{2,1},{3,0},{4,7},{5,6},{6,5},{7,4},{8,11},{9,10},{10,... | collective-permute-start | bytes 1966088 | tf_op jit(solution)/shard_map/ppermute | solution.py:743
  180.4 66.7 %collective-permute-start.13 = (bf16[2,10,128,128]{3,2,1,0:T(8,128)(2,1)}, bf16[2,10,128,128]{3,2,1,0:T(8,128)(2,1)}, u32[]{:S(2)}, u32[]{:S(2)}) collective-permute-start(bf16[2,10,128,128]{3,2,1,0:T(8,128)(2,1)} %get-tuple-element.95), channel_id=1, source_target_pairs={{0,1},{1,0},{2,3},{3,2},{4,5},{5,4},{6,7},{7,6},{8,9},{9,8},{10,11... | collective-permute-start | bytes 1966088 | tf_op jit(solution)/shard_map/ppermute | solution.py:743
  180.4 66.7 %collective-permute-start.14 = (bf16[2,10,128,128]{3,2,1,0:T(8,128)(2,1)}, bf16[2,10,128,128]{3,2,1,0:T(8,128)(2,1)}, u32[]{:S(2)}, u32[]{:S(2)}) collective-permute-start(bf16[2,10,128,128]{3,2,1,0:T(8,128)(2,1)} %get-tuple-element.96), channel_id=1, source_target_pairs={{0,2},{1,3},{2,0},{3,1},{4,6},{5,7},{6,4},{7,5},{8,10},{9,11},{10,... | collective-permute-start | bytes 1966088 | tf_op jit(solution)/shard_map/ppermute | solution.py:743
  181.6 65.5 %collective-permute-start.15 = (bf16[2,10,128,128]{3,2,1,0:T(8,128)(2,1)}, bf16[2,10,128,128]{3,2,1,0:T(8,128)(2,1)}, u32[]{:S(2)}, u32[]{:S(2)}) collective-permute-start(bf16[2,10,128,128]{3,2,1,0:T(8,128)(2,1)} %get-tuple-element.97), channel_id=1, source_target_pairs={{0,3},{1,2},{2,1},{3,0},{4,7},{5,6},{6,5},{7,4},{8,11},{9,10},{10,... | collective-permute-start | bytes 1966088 | tf_op jit(solution)/shard_map/ppermute | solution.py:743
  247.1 5.8 %copy-start.6 = (bf16[128,1024]{1,0:T(8,128)(2,1)S(1)}, bf16[128,1024]{1,0:T(8,128)(2,1)}, u32[]{:S(2)}) copy-start(bf16[128,1024]{1,0:T(8,128)(2,1)} %get-tuple-element.106) | copy-start | bytes 786436
  247.1 6.5 %copy-start.5 = (bf16[128,1024]{1,0:T(8,128)(2,1)S(1)}, bf16[128,1024]{1,0:T(8,128)(2,1)}, u32[]{:S(2)}) copy-start(bf16[128,1024]{1,0:T(8,128)(2,1)} %get-tuple-element.107) | copy-start | bytes 786436

commit v3 on v2

--- a/solution.py
+++ b/solution.py
@@ -145,7 +145,7 @@
 def gather_kernel(shards, tokens, cotangent, *refs):
     rows, factors, (wg, wu, wd), refs = refs[:3], refs[3:6], refs[6:9], refs[9:]
     tok_all, rg, ru, rd, row_table, factor_table, spot, both, *sems = refs
-    (z_send, z_recv, c_send, c_recv, x_send, x_recv, w_send, w_recv, y_send, y_recv, n_send, n_recv, s_send, s_recv, here) = sems
+    (z_send, z_recv, c_send, c_recv, x_send, x_recv, w_send, w_recv, y_send, y_recv, n_send, n_recv, s_send, s_recv, e_send, e_recv, here) = sems
     part, t, f = lax.axis_index("parts"), lax.axis_index("tensor"), lax.axis_index("fsdp")
     flip = [f, (f // 2) * 2 + 1 - f % 2, (f + 2) % 4, ((f + 2) % 4 // 2) * 2 + 1 - f % 2]
     count = rg.shape[2]
@@ -191,9 +191,14 @@
     def _():
         pl.semaphore_wait(barrier, 6)
 
-    def z_copy(way, src, x, own=False):
-        source = both if own else tok_all.at[0, src, x]
-        return to(ups[way], source, tok_all.at[0, src, x], z_send.at[way, src, x], z_recv.at[way, src, x])
+    def z_copy(way, src, x, own=False, hops=0):
+        place = tok_all.at[0, src, x]
+        if x == 1 and hops == last:
+            place = tok_all.at[0, src, x, 0]
+        return to(ups[way], both if own else place, place, z_send.at[way, src, x], z_recv.at[way, src, x])
+
+    def e_copy(src):
+        return to(across(2), tok_all.at[0, src, 0, 1], tok_all.at[0, src, 1, 1], e_send, e_recv)
 
     def c_copy(src, x, own=False):
         source = both if own else tok_all.at[0, src, x]
@@ -234,7 +239,7 @@
     for way in range(2):
         @pl.when(more[way])
         def _():
-            z_copy(way, t, 1).start()
+            z_copy(way, t, 1, hops=1).start()
     c_copy(t, 1).start()
 
     def arrive(step, x):
@@ -243,11 +248,17 @@
 
             @pl.when(src >= 0 if way == 0 else src <= last)
             def _():
-                z_copy(way, src, x).wait_recv()
+                z_copy(way, src, x, hops=step).wait_recv()
 
                 @pl.when(more[way])
                 def _():
-                    z_copy(way, src, x).start()
+                    z_copy(way, src, x, hops=step + 1).start()
+
+                if step == last:
+                    if x == 0:
+                        e_copy(src).start()
+                    else:
+                        e_copy(src).wait_recv()
 
                 c_copy(src, x).start()
 
@@ -273,7 +284,12 @@
             @pl.when(jnp.logical_and(src >= 0 if way == 0 else src <= last, more[way]))
             def _():
                 for x in range(2):
-                    z_copy(way, src, x, s == 0 and x == 0).wait_send()
+                    z_copy(way, src, x, s == 0 and x == 0, s + 1).wait_send()
+
+        @pl.when(t == last if way == 0 else t == 0)
+        def _():
+            e_copy(0 if way == 0 else last).wait_send()
+
     for src in range(shards):
         for x in range(2):
             c_copy(src, x).wait_send()
@@ -315,7 +331,7 @@
         out_specs=[anywhere] * 4 + [local] * 2 + [pl.BlockSpec(memory_space=pltpu.SMEM)],
         scratch_shapes=[
             pltpu.VMEM(both, bf),
-            dma(*z), dma(*z), dma(*c), dma(*c), one, one, dma(6), dma(6), dma(6), dma(6), dma(6), dma(6), dma(2, 3), dma(2, 3), one,
+            dma(*z), dma(*z), dma(*c), dma(*c), one, one, dma(6), dma(6), dma(6), dma(6), dma(6), dma(6), dma(2, 3), dma(2, 3), one, one, one,
         ],
         compiler_params=pltpu.CompilerParams(collective_id=0, has_side_effects=True),
     )(tokens, cotangent, *rows, *factors, *weights)
@@ -423,13 +439,12 @@
     gate_act = (grad_hidden * up_pre * sig * (1.0 + gate_pre * (1.0 - sig))).astype(jnp.bfloat16)
     up_act = (grad_hidden * act).astype(jnp.bfloat16)
     gate_act_ref[0], up_act_ref[0] = gate_act, up_act
-    for slot in range(slots):
-        span = slice(slot * blk, (slot + 1) * blk)
-        src, sub = slot // per_dev, slot % per_dev
-        g = dot(gate_sel[:, span].T, gate_act, NN) * entry(scale_ref, 0, slot, r)
-        grads[0][src][sub, 0] = g.astype(jnp.bfloat16)
-        g = dot(up_sel[:, span].T, up_act, NN) * entry(scale_ref, 1, slot, r)
-        grads[1][src][sub, 0] = g.astype(jnp.bfloat16)
+    for array, (sel, act) in enumerate(((gate_sel, gate_act), (up_sel, up_act))):
+        product = dot(act.T, sel[...], NN)
+        for slot in range(slots):
+            src, sub = slot // per_dev, slot % per_dev
+            g = product[:, slot * blk : (slot + 1) * blk] * entry(scale_ref, array, slot, r)
+            grads[array][src][sub, 0] = g.astype(jnp.bfloat16).T
 
 
 def late_kernel(dims, rows_ref, scale_ref, place_ref, *refs):
@@ -507,13 +522,15 @@
 
 def add_kernel(pairs, *refs):
     left, right, out, (held, load_sem, store_sem) = refs[:pairs], refs[pairs : 2 * pairs], refs[2 * pairs : 3 * pairs], refs[3 * pairs :]
-    loads = [pltpu.make_async_copy(a, held.at[0, m], load_sem.at[m]) for m, a in enumerate(left)]
-    stores = [pltpu.make_async_copy(held.at[1, m], c, store_sem.at[m]) for m, c in enumerate(out)]
-    for c in loads:
-        c.start()
+    loads = [[pltpu.make_async_copy(a, held.at[i, m], load_sem.at[i, m]) for m, a in enumerate(side)] for i, side in enumerate((left, right))]
+    stores = [pltpu.make_async_copy(held.at[2, m], c, store_sem.at[m]) for m, c in enumerate(out)]
     for m in reversed(range(pairs)):
-        loads[m].wait()
-        held[1, m] = (held[0, m].astype(jnp.float32) + right[m][...].astype(jnp.float32)).astype(held.dtype)
+        loads[0][m].start()
+        loads[1][m].start()
+    for m in reversed(range(pairs)):
+        loads[0][m].wait()
+        loads[1][m].wait()
+        held[2, m] = (held[0, m].astype(jnp.float32) + held[1, m].astype(jnp.float32)).astype(held.dtype)
         stores[m].start()
     for c in stores:
         c.wait()
@@ -521,15 +538,14 @@
 
 def add_pairs(left, right):
     pairs, unit = len(left), left[0]
-    stay, local = pl.BlockSpec(memory_space=pltpu.HBM), pl.BlockSpec(memory_space=pltpu.VMEM)
-    dma = pltpu.SemaphoreType.DMA((pairs,))
+    anywhere, dma = pl.BlockSpec(memory_space=pl.ANY), pltpu.SemaphoreType.DMA
     return pl.pallas_call(
         functools.partial(add_kernel, pairs),
-        in_specs=[stay] * pairs + [local] * pairs,
-        out_specs=[stay] * pairs,
+        in_specs=[anywhere] * (2 * pairs),
+        out_specs=[anywhere] * pairs,
         out_shape=[jax.ShapeDtypeStruct(unit.shape, unit.dtype)] * pairs,
-        scratch_shapes=[pltpu.VMEM((2, pairs) + unit.shape, unit.dtype), dma, dma],
-        compiler_params=pltpu.CompilerParams(vmem_limit_bytes=64_600_000),
+        scratch_shapes=[pltpu.VMEM((3, pairs) + unit.shape, unit.dtype), dma((2, pairs)), dma((pairs,))],
+        compiler_params=pltpu.CompilerParams(vmem_limit_bytes=66_400_000),
     )(*left, *right)
 
 

time: 256 us -> 246 us (0.961)
  Pallas kernels: 206 us -> 197 us
    pallas_call x3, Pallas kernels: 69.3 us -> 64.6 us  [columns(): pl.pallas_call(body, grid_spec=pltpu.PrefetchScalarGridSpec(num_scalar_pr...]
    pallas_call x1, Pallas kernels: 78.9 us -> 75.7 us  [gather(): pl.pallas_call(functools.partial(gather_kernel, shards), out_shape=[jax.S...]
  transfers between devices with their start and end apart: 16 -> 16, of which waited for: 3 -> 4; matrix products, arithmetic and copies ran while one was open for 0% -> 0% of each run, Pallas kernels for 38% -> 37%
where the time goes in v3:
time: 246 us; the launch traced here: 245 us
  Pallas kernels  197 us (80%)
  waiting for transfers between devices  32.9 us (13%)
  starting transfers between devices  12.4 us (5%)
    pallas_call x1, Pallas kernels, gather(): pl.pallas_call(functools.partial(gather_kernel, shards), out_shape=[jax.S...  75.7 us
    pallas_call x3, Pallas kernels, columns(): pl.pallas_call(body, grid_spec=pltpu.PrefetchScalarGridSpec(num_scalar_pr...  64.6 us
    pallas_call x1, Pallas kernels, reduce(): pl.pallas_call(functools.partial(reduce_kernel, shards), out_shape=[jax.S...  48 us
    ppermute x16, waiting for transfers between devices, swap(): lax.ppermute(value, axis, [(i, i ^ flip) for i in range(lax.axis_size(axi...  32.9 us
    ppermute x16, starting transfers between devices, swap(): lax.ppermute(value, axis, [(i, i ^ flip) for i in range(lax.axis_size(axi...  12.4 us
    pallas_call x1, Pallas kernels, home(): pl.pallas_call(functools.partial(home_kernel, arrays), grid_spec=pltpu.Pr...  5.73 us
  transfers between devices with their start and end apart: 16, of which 4 were waited for; matrix products, arithmetic and copies ran while one was open for 0% of the time, Pallas kernels for 37%

profile of v3, /device:TPU:0, one launch (start us, length us, event | category | flops | bytes accessed | tf_op | source)
XLA Modules:
  0.0 244.6 jit_solution(9034621052964777155)
XLA Ops:
  0.6 75.7 %shard_map.146 = (bf16[2,4,2,2,8,128,128]{6,5,4,3,2,1,0:T(8,128)(2,1)}, bf16[3,2,10,128,128]{4,3,2,1,0:T(8,128)(2,1)}, bf16[3,2,10,128,128]{4,3,2,1,0:T(8,128)(2...) custom-call(bf16[128,1024]{1,0:T(8,128)(2,1)} %tokens.1, ...), custom_call_target="tpu_custom_call" | custom-call | tf_op jit(solution)/shard_map/pallas_call | solution.py:321
  76.4 25.6 %shard_map.147 = (bf16[2,10,128,128]{3,2,1,0:T(8,128)(2,1)}, bf16[2,10,128,128]{3,2,1,0:T(8,128)(2,1)}, bf16[2,10,128,128]{3,2,1,0:T(8,128)(2,1)}, bf16[2,10,128...) custom-call(s32[4,3,2,40]{3,2,1,0:T(2,128)} %get-tuple-element.53.ro, ...), custom_call_target="tpu_custom_call" | custom-call | flops 5368709120 | bytes 41943040 | tf_op jit(solution)/shard_map/pallas_call | solution.py:512
  102.0 0.4 collective-permute-start
  102.4 0.1 collective-permute-start.1
  102.6 0.4 collective-permute-start.2
  102.9 0.1 collective-permute-start.3
  103.1 0.4 collective-permute-start.4
  103.4 0.7 collective-permute-done.refs_4_
  104.2 1.5 collective-permute-start.5
  105.6 0.0 collective-permute-done.1.refs_5_
  105.6 0.9 collective-permute-start.6
  106.5 0.1 collective-permute-done.3.refs_7_
  106.6 3.2 %shard_map.148 = (bf16[2,8,128,128]{3,2,1,0:T(8,128)(2,1)}, bf16[2,8,128,128]{3,2,1,0:T(8,128)(2,1)}, bf16[2,8,128,128]{3,2,1,0:T(8,128)(2,1)}, bf16[2,8,128,128]{3,2,1,0:T(8,128)(2,1)}) custom-call(bf16[2,8,128,128]{3,2,1,0:T(8,128)(2,1)} %get-tuple-element.60.refs_0_, bf16[2,8,128,128]{3,2,1,0:T(8,128)(2,1)} %get-tuple-element.61.refs_1_, ...), custom_call_target="tpu_custom_call" | custom-call | tf_op jit(solution)/shard_map/pallas_call | solution.py:542
  109.8 22.0 %shard_map.149 = (bf16[2,10,128,128]{3,2,1,0:T(8,128)(2,1)}, bf16[2,10,128,128]{3,2,1,0:T(8,128)(2,1)}, bf16[2,10,128,128]{3,2,1,0:T(8,128)(2,1)}, bf16[2,10,128...) custom-call(s32[4,3,2,40]{3,2,1,0:T(2,128)} %get-tuple-element.53.ro, ...), custom_call_target="tpu_custom_call" | custom-call | flops 4026531840 | bytes 41943040 | tf_op jit(solution)/shard_map/pallas_call | solution.py:512
  131.7 0.4 collective-permute-start.10
  132.2 0.0 collective-permute-done.4.refs_7_
  132.2 3.0 %collective-permute-start.8 = (bf16[2,8,128,128]{3,2,1,0:T(8,128)(2,1)S(1)}, bf16[2,8,128,128]{3,2,1,0:T(8,128)(2,1)}, u32[]{:S(2)}, u32[]{:S(2)}) collective-permute-start(bf16[2,8,128,128]{3,2,1,0:T(8,128)(2,1)S(1)} %copy-done.5), channel_id=1, source_target_pairs={{0,8},{4,12},{8,0},{12,4},{1,9},{5,13},{9,1},{13,5},{2,10},{6,14},... | collective-permute-start | bytes 1572872 | tf_op jit(solution)/shard_map/ppermute | solution.py:759
  135.2 0.0 collective-permute-done.5.refs_8_
  135.2 1.4 collective-permute-start.9
  136.6 1.5 collective-permute-start.11
  138.0 18.8 %collective-permute-done.7.refs_0_ = bf16[2,8,128,128]{3,2,1,0:T(8,128)(2,1)S(1)} collective-permute-done((bf16[2,8,128,128]{3,2,1,0:T(8,128)(2,1)S(1)}, bf16[2,8,128,128]{3,2,1,0:T(8,128)(2,1)S(1)}, u32[]{:S(2)}, u32[]{:S(2)}) %collective-permute-start.7) | collective-permute-done | bytes 524320 | tf_op jit(solution)/shard_map/ppermute | solution.py:759
  156.8 0.4 collective-permute-start.12
  157.3 13.3 %collective-permute-done.8.refs_1_ = bf16[2,8,128,128]{3,2,1,0:T(8,128)(2,1)} collective-permute-done((bf16[2,8,128,128]{3,2,1,0:T(8,128)(2,1)S(1)}, bf16[2,8,128,128]{3,2,1,0:T(8,128)(2,1)}, u32[]{:S(2)}, u32[]{:S(2)}) %collective-permute-start.8) | collective-permute-done | bytes 524320 | tf_op jit(solution)/shard_map/ppermute | solution.py:759
  170.6 1.5 collective-permute-start.14
  172.1 0.4 collective-permute-start.15
  172.5 17.0 %shard_map.150 = (bf16[4,2,8,128,128]{4,3,2,1,0:T(8,128)(2,1)}, bf16[4,2,8,128,128]{4,3,2,1,0:T(8,128)(2,1)}, bf16[2,4,10,128,128]{4,3,2,1,0:T(8,128)(2,1)}) custom-call(s32[4,3,2,40]{3,2,1,0:T(2,128)} %get-tuple-element.53.rows_ref, f32[4,3,2,40]{3,2,1,0:T(2,128)} %get-tuple-element.54.scale_ref, s32[2]{0:T(128)} %get-tuple-element.55.place_ref, ...), custom_call_target="tpu_custom_call" | custom-call | flops 2684354560 | bytes 41943040 | tf_op jit(solution)/shard_map/pallas_call | solution.py:512
  189.4 48.0 %shard_map.151 = (bf16[128,1024]{1,0:T(8,128)(2,1)}, bf16[128,1024]{1,0:T(8,128)(2,1)}) custom-call(bf16[4,2,8,128,128]{4,3,2,1,0:T(8,128)(2,1)} %get-tuple-element.82.own, bf16[4,2,8,128,128]{4,3,2,1,0:T(8,128)(2,1)} %get-tuple-element.83.other, bf16[2,8,128,128]{3,2,1,0:T(8,128)(2,1)} %get-tuple-element.84.first, bf16[2,8,128,128]{3,2,1,0:T(8,128)(2,1)} %copy-done, ...), custom_call_target="tpu_custom_call" | custom-call | tf_op jit(solution)/shard_map/pallas_call | solution.py:701
  237.4 0.0 collective-permute-done.11.refs_2_
  237.4 0.0 collective-permute-done.14.refs_6_
  237.5 5.7 %shard_map.152 = (bf16[2,40,128,128]{3,2,1,0:T(8,128)(2,1)}, bf16[2,40,128,128]{3,2,1,0:T(8,128)(2,1)}) custom-call(s32[2]{0:T(128)} %get-tuple-element.55.place_ref, bf16[2,10,128,128]{3,2,1,0:T(8,128)(2,1)} %get-tuple-element.90.refs_0_, bf16[2,10,128,128]{3,2,1,0:T(8,128)(2,1)} %collective-permute-done.10.refs_1_, ...), custom_call_target="tpu_custom_call" | custom-call | tf_op jit(solution)/shard_map/pallas_call | solution.py:744
  243.2 0.7 copy.18
  243.9 0.7 copy.19
  (23 shorter events, 0.1 us)
Async XLA Ops:
  102.0 2.2 collective-permute-start
  102.4 3.2 %collective-permute-start.1 = (bf16[2,8,128,128]{3,2,1,0:T(8,128)(2,1)}, bf16[2,8,128,128]{3,2,1,0:T(8,128)(2,1)}, u32[]{:S(2)}, u32[]{:S(2)}) collective-permute-start(bf16[2,8,128,128]{3,2,1,0:T(8,128)(2,1)} %get-tuple-element.65), channel_id=1, source_target_pairs={{0,1},{1,0},{2,3},{3,2},{4,5},{5,4},{6,7},{7,6},{8,9},{9,8},{10,11... | collective-permute-start | bytes 1572872 | tf_op jit(solution)/shard_map/ppermute | solution.py:759
  102.6 3.9 %collective-permute-start.2 = (bf16[2,8,128,128]{3,2,1,0:T(8,128)(2,1)}, bf16[2,8,128,128]{3,2,1,0:T(8,128)(2,1)}, u32[]{:S(2)}, u32[]{:S(2)}) collective-permute-start(bf16[2,8,128,128]{3,2,1,0:T(8,128)(2,1)} %get-tuple-element.66), channel_id=1, source_target_pairs={{0,1},{1,0},{2,3},{3,2},{4,5},{5,4},{6,7},{7,6},{8,9},{9,8},{10,11... | collective-permute-start | bytes 1572872 | tf_op jit(solution)/shard_map/ppermute | solution.py:759
  102.9 3.6 %collective-permute-start.3 = (bf16[2,8,128,128]{3,2,1,0:T(8,128)(2,1)}, bf16[2,8,128,128]{3,2,1,0:T(8,128)(2,1)}, u32[]{:S(2)}, u32[]{:S(2)}) collective-permute-start(bf16[2,8,128,128]{3,2,1,0:T(8,128)(2,1)} %get-tuple-element.67), channel_id=1, source_target_pairs={{0,1},{1,0},{2,3},{3,2},{4,5},{5,4},{6,7},{7,6},{8,9},{9,8},{10,11... | collective-permute-start | bytes 1572872 | tf_op jit(solution)/shard_map/ppermute | solution.py:759
  103.1 29.1 %collective-permute-start.4 = (bf16[2,10,128,128]{3,2,1,0:T(8,128)(2,1)}, bf16[2,10,128,128]{3,2,1,0:T(8,128)(2,1)}, u32[]{:S(2)}, u32[]{:S(2)}) collective-permute-start(bf16[2,10,128,128]{3,2,1,0:T(8,128)(2,1)} %get-tuple-element.79), channel_id=1, source_target_pairs={{0,1},{1,0},{2,3},{3,2},{4,5},{5,4},{6,7},{7,6},{8,9},{9,8},{10,11... | collective-permute-start | bytes 1966088 | tf_op jit(solution)/shard_map/ppermute | solution.py:759
  104.2 2.4 copy-start.1
  104.2 31.0 %collective-permute-start.5 = (bf16[2,10,128,128]{3,2,1,0:T(8,128)(2,1)}, bf16[2,10,128,128]{3,2,1,0:T(8,128)(2,1)}, u32[]{:S(2)}, u32[]{:S(2)}) collective-permute-start(bf16[2,10,128,128]{3,2,1,0:T(8,128)(2,1)} %get-tuple-element.80), channel_id=1, source_target_pairs={{0,2},{1,3},{2,0},{3,1},{4,6},{5,7},{6,4},{7,5},{8,10},{9,11},{10,... | collective-permute-start | bytes 1966088 | tf_op jit(solution)/shard_map/ppermute | solution.py:759
  105.6 30.9 %collective-permute-start.6 = (bf16[2,10,128,128]{3,2,1,0:T(8,128)(2,1)}, bf16[2,10,128,128]{3,2,1,0:T(8,128)(2,1)}, u32[]{:S(2)}, u32[]{:S(2)}) collective-permute-start(bf16[2,10,128,128]{3,2,1,0:T(8,128)(2,1)} %get-tuple-element.81), channel_id=1, source_target_pairs={{0,3},{1,2},{2,1},{3,0},{4,7},{5,6},{6,5},{7,4},{8,11},{9,10},{10,... | collective-permute-start | bytes 1966088 | tf_op jit(solution)/shard_map/ppermute | solution.py:759
  109.7 22.4 %copy-start.6 = (bf16[2,8,128,128]{3,2,1,0:T(8,128)(2,1)S(1)}, bf16[2,8,128,128]{3,2,1,0:T(8,128)(2,1)}, u32[]{:S(2)}) copy-start(bf16[2,8,128,128]{3,2,1,0:T(8,128)(2,1)} %get-tuple-element.85) | copy-start | bytes 1572868
  109.7 22.4 %copy-start.5 = (bf16[2,8,128,128]{3,2,1,0:T(8,128)(2,1)S(1)}, bf16[2,8,128,128]{3,2,1,0:T(8,128)(2,1)}, u32[]{:S(2)}) copy-start(bf16[2,8,128,128]{3,2,1,0:T(8,128)(2,1)} %get-tuple-element.86) | copy-start | bytes 1572868
  109.7 25.4 %copy-start.4 = (bf16[2,8,128,128]{3,2,1,0:T(8,128)(2,1)S(1)}, bf16[2,8,128,128]{3,2,1,0:T(8,128)(2,1)}, u32[]{:S(2)}) copy-start(bf16[2,8,128,128]{3,2,1,0:T(8,128)(2,1)} %get-tuple-element.87) | copy-start | bytes 1572868
  131.7 40.3 %collective-permute-start.10 = (bf16[2,10,128,128]{3,2,1,0:T(8,128)(2,1)}, bf16[2,10,128,128]{3,2,1,0:T(8,128)(2,1)}, u32[]{:S(2)}, u32[]{:S(2)}) collective-permute-start(bf16[2,10,128,128]{3,2,1,0:T(8,128)(2,1)} %get-tuple-element.91), channel_id=1, source_target_pairs={{0,1},{1,0},{2,3},{3,2},{4,5},{5,4},{6,7},{7,6},{8,9},{9,8},{10,11... | collective-permute-start | bytes 1966088 | tf_op jit(solution)/shard_map/ppermute | solution.py:759
  132.2 24.7 %collective-permute-start.7 = (bf16[2,8,128,128]{3,2,1,0:T(8,128)(2,1)S(1)}, bf16[2,8,128,128]{3,2,1,0:T(8,128)(2,1)S(1)}, u32[]{:S(2)}, u32[]{:S(2)}) collective-permute-start(bf16[2,8,128,128]{3,2,1,0:T(8,128)(2,1)S(1)} %copy-done.6), channel_id=1, source_target_pairs={{0,4},{4,0},{8,12},{12,8},{1,5},{5,1},{9,13},{13,9},{2,6},{6,2},{1... | collective-permute-start | bytes 1572872 | tf_op jit(solution)/shard_map/ppermute | solution.py:759
  132.2 38.4 %collective-permute-start.8 = (bf16[2,8,128,128]{3,2,1,0:T(8,128)(2,1)S(1)}, bf16[2,8,128,128]{3,2,1,0:T(8,128)(2,1)}, u32[]{:S(2)}, u32[]{:S(2)}) collective-permute-start(bf16[2,8,128,128]{3,2,1,0:T(8,128)(2,1)S(1)} %copy-done.5), channel_id=1, source_target_pairs={{0,8},{4,12},{8,0},{12,4},{1,9},{5,13},{9,1},{13,5},{2,10},{6,14},... | collective-permute-start | bytes 1572872 | tf_op jit(solution)/shard_map/ppermute | solution.py:759
  135.2 35.4 %collective-permute-start.9 = (bf16[2,8,128,128]{3,2,1,0:T(8,128)(2,1)S(1)}, bf16[2,8,128,128]{3,2,1,0:T(8,128)(2,1)}, u32[]{:S(2)}, u32[]{:S(2)}) collective-permute-start(bf16[2,8,128,128]{3,2,1,0:T(8,128)(2,1)S(1)} %copy-done.4), channel_id=1, source_target_pairs={{0,12},{4,8},{8,4},{12,0},{1,13},{5,9},{9,5},{13,1},{2,14},{6,10},... | collective-permute-start | bytes 1572872 | tf_op jit(solution)/shard_map/ppermute | solution.py:759
  136.6 100.8 %collective-permute-start.11 = (bf16[2,10,128,128]{3,2,1,0:T(8,128)(2,1)}, bf16[2,10,128,128]{3,2,1,0:T(8,128)(2,1)}, u32[]{:S(2)}, u32[]{:S(2)}) collective-permute-start(bf16[2,10,128,128]{3,2,1,0:T(8,128)(2,1)} %get-tuple-element.92), channel_id=1, source_target_pairs={{0,2},{1,3},{2,0},{3,1},{4,6},{5,7},{6,4},{7,5},{8,10},{9,11},{10,... | collective-permute-start | bytes 1966088 | tf_op jit(solution)/shard_map/ppermute | solution.py:759
  156.8 32.6 %copy-start = (bf16[2,8,128,128]{3,2,1,0:T(8,128)(2,1)}, bf16[2,8,128,128]{3,2,1,0:T(8,128)(2,1)S(1)}, u32[]{:S(2)}) copy-start(bf16[2,8,128,128]{3,2,1,0:T(8,128)(2,1)S(1)} %collective-permute-done.7.refs_0_) | copy-start | bytes 1572868
  156.8 80.6 %collective-permute-start.12 = (bf16[2,10,128,128]{3,2,1,0:T(8,128)(2,1)}, bf16[2,10,128,128]{3,2,1,0:T(8,128)(2,1)}, u32[]{:S(2)}, u32[]{:S(2)}) collective-permute-start(bf16[2,10,128,128]{3,2,1,0:T(8,128)(2,1)} %get-tuple-element.93), channel_id=1, source_target_pairs={{0,3},{1,2},{2,1},{3,0},{4,7},{5,6},{6,5},{7,4},{8,11},{9,10},{10,... | collective-permute-start | bytes 1966088 | tf_op jit(solution)/shard_map/ppermute | solution.py:759
  170.6 66.9 %collective-permute-start.13 = (bf16[2,10,128,128]{3,2,1,0:T(8,128)(2,1)}, bf16[2,10,128,128]{3,2,1,0:T(8,128)(2,1)}, u32[]{:S(2)}, u32[]{:S(2)}) collective-permute-start(bf16[2,10,128,128]{3,2,1,0:T(8,128)(2,1)} %get-tuple-element.95), channel_id=1, source_target_pairs={{0,1},{1,0},{2,3},{3,2},{4,5},{5,4},{6,7},{7,6},{8,9},{9,8},{10,11... | collective-permute-start | bytes 1966088 | tf_op jit(solution)/shard_map/ppermute | solution.py:759
  170.6 66.9 %collective-permute-start.14 = (bf16[2,10,128,128]{3,2,1,0:T(8,128)(2,1)}, bf16[2,10,128,128]{3,2,1,0:T(8,128)(2,1)}, u32[]{:S(2)}, u32[]{:S(2)}) collective-permute-start(bf16[2,10,128,128]{3,2,1,0:T(8,128)(2,1)} %get-tuple-element.96), channel_id=1, source_target_pairs={{0,2},{1,3},{2,0},{3,1},{4,6},{5,7},{6,4},{7,5},{8,10},{9,11},{10,... | collective-permute-start | bytes 1966088 | tf_op jit(solution)/shard_map/ppermute | solution.py:759
  172.1 65.4 %collective-permute-start.15 = (bf16[2,10,128,128]{3,2,1,0:T(8,128)(2,1)}, bf16[2,10,128,128]{3,2,1,0:T(8,128)(2,1)}, u32[]{:S(2)}, u32[]{:S(2)}) collective-permute-start(bf16[2,10,128,128]{3,2,1,0:T(8,128)(2,1)} %get-tuple-element.97), channel_id=1, source_target_pairs={{0,3},{1,2},{2,1},{3,0},{4,7},{5,6},{6,5},{7,4},{8,11},{9,10},{10,... | collective-permute-start | bytes 1966088 | tf_op jit(solution)/shard_map/ppermute | solution.py:759
  237.5 5.8 %copy-start.3 = (bf16[128,1024]{1,0:T(8,128)(2,1)S(1)}, bf16[128,1024]{1,0:T(8,128)(2,1)}, u32[]{:S(2)}) copy-start(bf16[128,1024]{1,0:T(8,128)(2,1)} %get-tuple-element.106) | copy-start | bytes 786436
  237.5 6.5 %copy-start.2 = (bf16[128,1024]{1,0:T(8,128)(2,1)S(1)}, bf16[128,1024]{1,0:T(8,128)(2,1)}, u32[]{:S(2)}) copy-start(bf16[128,1024]{1,0:T(8,128)(2,1)} %get-tuple-element.107) | copy-start | bytes 786436
